TPU v7x, 256 devices: a whole 4x4x8 slice. The times are simulated.
256 devices in a mesh: replica: 64 (over z_lo, y, x, core), tensor: 4 (over z_hi).
Axes of the slice: x: 4, y: 4, z: 8 (z_hi: 4, z_lo: 2; z = z_hi * 2 + z_lo), core: 2. Of those that a mesh axis runs over, the one named last changes fastest.
Arguments:
- x_in: bfloat16 [32768, 4096], P('replica', 'tensor'), may hold values from -6 to 6
- gate_z: bfloat16 [32768, 4096], P('replica', 'tensor'), may hold values from -6 to 6
- b_proj: bfloat16 [32768, 1024], P('replica', 'tensor'), may hold values from -2 to 2
- c_proj: bfloat16 [32768, 1024], P('replica', 'tensor'), may hold values from -2 to 2
- dt_raw: float32 [32768, 64], P('replica', 'tensor'), may hold values from -5 to 5
- a_log: float32 [64], P('tensor'), may hold values from 0 to 2.77
- dt_bias: float32 [64], P('tensor'), may hold values from -6 to -2
- skip_d: float32 [64], P('tensor'), may hold values from 0.5 to 1.5
- norm_gain: float32 [4096], P('tensor'), may hold values from 0.5 to 1.5
- out_weight: bfloat16 [64, 2048, 4096], P('replica', None, 'tensor'), may hold values from -0.25 to 0.25
- global_weight: float32 [2048, 4096], P('replica', 'tensor'), may hold values from -0.09375 to 0.09375
- momentum: float32 [2048, 4096], P('replica', 'tensor'), may hold values from -0.04 to 0.04
- target: bfloat16 [32768, 2048], P(('replica', 'tensor')), may hold values from -6 to 6
Outputs:
- grad_x: bfloat16 [32768, 4096], P('replica', 'tensor')
- new_weight: bfloat16 [2048, 4096], P(None, 'tensor')
- new_global: float32 [2048, 4096], P('replica', 'tensor')
- new_momentum: float32 [2048, 4096], P('replica', 'tensor')
All inputs are finite; a program needn't handle non-finite values.
Results may differ from a plain program's by a relative error of at most 0.0085.
Values may be sent and summed in bfloat16 or wider, within the bound.
A program may use at most 128 MiB of HBM per device.

v0:
```python
import jax
import jax.numpy as jnp
from jax import lax
from jax.sharding import Mesh
from jax.sharding import PartitionSpec as P

HEAD_DIM = 64
STATE = 128
SPAN = 256
REPLICA = ("replica_0", "replica_1", "replica_2", "replica_3")
REPLICA_TENSOR = ("replica_0", "replica_1", "replica_2", "replica_3", "tensor")


inner_rate = 0.001
outer_rate = 0.7
outer_beta = 0.9
clip_rms = 0.005


def split_up(value, dim, length):
    shape = value.shape
    pieces = value.reshape(*shape[:dim], length, shape[dim] // length, *shape[dim + 1 :])
    return jnp.moveaxis(pieces, dim, 0)


def sum_at_owner(value, axis, dim):
    length = lax.axis_size(axis)
    pieces = lax.all_to_all(split_up(value, dim, length), axis, 0, 0, tiled=True)
    return jnp.sum(pieces, axis=0)


def from_everyone(value, axis):
    length = lax.axis_size(axis)
    return lax.all_to_all(
        jnp.broadcast_to(value[None], (length, *value.shape)), axis, 0, 0, tiled=True
    )


def in_order(pieces, dim):
    shape = list(pieces.shape[1:])
    shape[dim] *= pieces.shape[0]
    return jnp.moveaxis(pieces, 0, dim).reshape(shape)


def gather_directly(value, axis, dim):
    pieces = from_everyone(value, axis)
    return in_order(pieces, dim)


def summed_rows(value, axes, dim):
    far, near = axes
    pieces = split_up(value, dim, lax.axis_size(far))
    nearer = sum_at_owner(pieces, near, dim + 1)
    arrived = lax.all_to_all(nearer, far, split_axis=0, concat_axis=0, tiled=True)
    return arrived.sum(axis=0)


def by_axis(value, axes):
    for axis in axes:
        value = lax.psum(value, axis)
    return value


def whole_of(value, axes, dim):
    far, near = axes
    pieces = from_everyone(from_everyone(value, far), near)
    return in_order(pieces.swapaxes(0, 1).reshape(-1, *value.shape), dim)


def gated_ssd(inputs_f, gate_z, b_proj, c_proj, dt_raw, a_log, dt_bias, skip_d, norm_gain):
    tokens = inputs_f.shape[0]
    head_count = a_log.shape[0]
    group_count = b_proj.shape[1] // STATE
    per_group = head_count // group_count
    block_count = tokens // SPAN
    values = inputs_f.reshape(block_count, SPAN, group_count, per_group, HEAD_DIM)
    step_size = jax.nn.softplus(dt_raw + dt_bias).reshape(block_count, SPAN, group_count, per_group)
    log_decay = (-jnp.exp(a_log)).reshape(group_count, per_group) * step_size
    cum_decay = jnp.cumsum(log_decay, axis=1)
    key_proj = b_proj.astype(jnp.float32).reshape(block_count, SPAN, group_count, STATE)
    query_proj = c_proj.astype(jnp.float32).reshape(block_count, SPAN, group_count, STATE)
    scores = jnp.einsum("clgn,csgn->cgls", query_proj, key_proj)
    cumulative = cum_decay.transpose(0, 2, 3, 1)
    gap_decay = cumulative[..., :, None] - cumulative[..., None, :]
    causal_mask = jnp.tril(jnp.ones((SPAN, SPAN), dtype=bool))
    decay_table = jnp.where(causal_mask, jnp.exp(jnp.where(causal_mask, gap_decay, 0.0)), 0.0)
    weights = scores[:, :, None] * decay_table * step_size.transpose(0, 2, 3, 1)[..., None, :]
    inside = jnp.einsum("cgrls,csgrp->clgrp", weights, values)
    tail_weight = jnp.exp(cum_decay[:, -1:] - cum_decay) * step_size
    states = jnp.einsum("csgn,csgr,csgrp->cgrpn", key_proj, tail_weight, values)
    span_fade = jnp.exp(cum_decay[:, -1])

    def carry_state(carried, inputs_pair):
        fade_now, state_now = inputs_pair
        return (fade_now[..., None, None] * carried + state_now, carried)

    _, entering = lax.scan(
        carry_state, jnp.zeros(states.shape[1:], jnp.float32), (span_fade, states)
    )
    outside = jnp.einsum("clgn,cgrpn->clgrp", query_proj, entering) * jnp.exp(cum_decay)[..., None]
    ssd_out = inside + outside + skip_d.reshape(group_count, per_group)[..., None] * values
    width = per_group * HEAD_DIM
    gated_vals = ssd_out.reshape(tokens, group_count, width) * jax.nn.silu(
        gate_z.astype(jnp.float32)
    ).reshape(tokens, group_count, width)
    inv_norm = lax.rsqrt(jnp.mean(gated_vals * gated_vals, axis=-1, keepdims=True) + 1e-05)
    return (gated_vals * inv_norm).reshape(tokens, head_count * HEAD_DIM) * norm_gain


def shards(
    x_in,
    gate_z,
    b_proj,
    c_proj,
    dt_raw,
    a_log,
    dt_bias,
    skip_d,
    norm_gain,
    out_weight,
    global_weight,
    momentum,
    target,
):
    local_weight = out_weight[0]

    def forward(inputs_f):
        return gated_ssd(
            inputs_f, gate_z, b_proj, c_proj, dt_raw, a_log, dt_bias, skip_d, norm_gain
        )

    normed_f, pull_back = jax.vjp(forward, x_in.astype(jnp.float32))
    normed = normed_f.astype(jnp.bfloat16)
    layer_part = sum_at_owner(
        lax.dot_general(
            normed, local_weight, (((1,), (1,)), ((), ())), preferred_element_type=jnp.float32
        ),
        "tensor",
        0,
    )
    cotangent_part = (layer_part - target.astype(jnp.float32)).astype(jnp.bfloat16)
    cotangent = gather_directly(cotangent_part, "tensor", 0)
    d_normed = jnp.dot(cotangent, local_weight, preferred_element_type=jnp.float32)
    grad_input = pull_back(d_normed)[0]
    weight_grad = lax.dot_general(
        cotangent, normed, (((0,), (0,)), ((), ())), preferred_element_type=jnp.float32
    )
    own_rows = local_weight.astype(jnp.float32)
    whole_term = own_rows - inner_rate * weight_grad
    summed = summed_rows(whole_term, (("replica_0", "replica_1", "replica_2"), "replica_3"), 0)
    replicas = lax.axis_size(REPLICA)
    delta = global_weight - summed / replicas
    square_sum = by_axis(jnp.sum(delta * delta), REPLICA_TENSOR)
    entry_count = delta.shape[0] * delta.shape[1] * replicas * lax.axis_size("tensor")
    factor = jnp.minimum(1.0, clip_rms / jnp.sqrt(square_sum / entry_count + 1e-06))
    clipped = factor * delta
    new_momentum = outer_beta * momentum + clipped
    new_global = global_weight - outer_rate * (clipped + outer_beta * new_momentum)
    new_weight = whole_of(
        new_global.astype(jnp.bfloat16), (("replica_0", "replica_1", "replica_2"), "replica_3"), 0
    )
    return (grad_input.astype(jnp.bfloat16), new_weight, new_global, new_momentum)


def solution(mesh):
    torus = Mesh(
        mesh.devices.reshape(2, 4, 4, 2, mesh.shape["tensor"]),
        ("replica_0", "replica_1", "replica_2", "replica_3", "tensor"),
    )
    in_specs = (
        P(REPLICA, "tensor"),
        P(REPLICA, "tensor"),
        P(REPLICA, "tensor"),
        P(REPLICA, "tensor"),
        P(REPLICA, "tensor"),
        P("tensor"),
        P("tensor"),
        P("tensor"),
        P("tensor"),
        P(REPLICA, None, "tensor"),
        P(REPLICA, "tensor"),
        P(REPLICA, "tensor"),
        P(REPLICA_TENSOR, None),
    )
    out_specs = (
        P(REPLICA, "tensor"),
        P(None, "tensor"),
        P(REPLICA, "tensor"),
        P(REPLICA, "tensor"),
    )
    return jax.shard_map(
        shards, mesh=torus, in_specs=in_specs, out_specs=out_specs, check_vma=False
    )
```

profile of v0, /device:TPU:1, one launch (start us, length us, event | category | flops | bytes accessed | tf_op | source)
XLA Modules:
  0.0 401.9 jit_solution(17653172280144386428)
XLA Ops:
  14.9 4.0 reshape.129
  18.9 3.6 copy.201
  30.0 4.3 %multiply_reduce_fusion.1 = (f32[2,256,2]{1,2,0:T(2,128)S(1)}, f32[2,256,2,8,64]{1,4,3,2,0:T(8,128)S(1)}) fusion(f32[2,256,2,8,64]{1,0,4,3,2:T(2,128)S(1)} %copy-done.4, bf16[2,256,2,8,64]{1,4,3,2,0:T(8,128)(2,1)S(1)} %copy-done.6, f32[2,8]{1,0:T(2,128)S(1)} %mul.205, f32[2,256,2,8]{1,3,2,0:T(8,128)S(1)} %get-tuple-element.231, ...), kind=kOutput, calls=%fused_computation.52 | convolution fusion | flops 283114496 | bytes 8556608 | tf_op jit(solution)/shard_map/jvp(cgrls,csgrp->clgrp)/dot_general | solution.py:88
  37.0 3.8 copy.233
  40.8 4.9 %reshape.126 = f32[512,1024]{1,0:T(8,128)} reshape(f32[2,256,2,8,64]{4,3,2,1,0:T(8,128)} %copy.233) | data formatting | bytes 4194304 | tf_op jit(solution)/shard_map/jvp()/reshape | solution.py:103
  45.8 3.2 multiply_convert_fusion
  49.2 2.4 fusion.3
  51.6 101.8 %all_to_all.32 = f32[4,128,2048]{2,1,0:T(8,128)} all-to-all(f32[4,128,2048]{2,1,0:T(8,128)S(1)} %fusion.3), channel_id=1, replica_groups=mesh['replica_0'=2,'replica_1'=4,'replica_2'=4,'replica_3'=2,'tensor'=4]..., dimensions={0} | all-to-all | bytes 8388608 | tf_op jit(solution)/shard_map/all_to_all | solution.py:28
  153.5 2.6 reduce_sum.61
  157.5 42.8 %all_to_all.33 = bf16[4,128,2048]{2,1,0:T(8,128)(2,1)S(1)} all-to-all(bf16[4,128,2048]{2,1,0:T(8,128)(2,1)S(1)} %broadcast_in_dim.68), channel_id=1, replica_groups=mesh['replica_0'=2,'replica_1'=4,'replica_2'=4,'replica_3'=2,'tensor'=4]..., dimensions={0} | all-to-all | bytes 4194304 | tf_op jit(solution)/shard_map/all_to_all | solution.py:34
  200.3 2.5 multiply_subtract_fusion
  204.5 17.6 %all_to_all.30 = f32[2,32,32,1024]{3,2,1,0:T(8,128)} all-to-all(f32[2,32,32,1024]{3,2,1,0:T(8,128)S(1)} %bitcast.133), channel_id=1, replica_groups=mesh['replica_0'=2,'replica_1'=4,'replica_2'=4,'replica_3'=2,'tensor'=4]..., dimensions={0} | all-to-all | bytes 16777216 | tf_op jit(solution)/shard_map/all_to_all | solution.py:28
  222.2 6.7 %reduce_sum.64 = f32[32,32,1024]{2,1,0:T(8,128)} reduce(f32[2,32,32,1024]{3,2,1,0:T(8,128)} %all_to_all.30, f32[]{:T(128)} %constant.79.clone.1), dimensions={0}, to_apply=%region_9.10 | reduce | flops 1048576 | bytes 12582916 | tf_op jit(solution)/shard_map/reduce_sum | solution.py:29
  228.9 62.3 %all_to_all.34 = f32[32,32,1024]{2,1,0:T(8,128)} all-to-all(f32[32,32,1024]{2,1,0:T(8,128)} %reduce_sum.64), channel_id=1, replica_groups=mesh['replica_0'=2,'replica_1'=4,'replica_2'=4,'replica_3'=2,'tensor'=4]..., dimensions={0} | all-to-all | bytes 8388608 | tf_op jit(solution)/shard_map/all_to_all | solution.py:54
  291.2 2.5 reduce_sum.65
  294.3 4.4 %psum.35 = f32[]{:T(128)} all-reduce(f32[]{:T(128)} %multiply_reduce_fusion.2), channel_id=1, replica_groups=mesh['replica_0'=2,'replica_1'=4,'replica_2'=4,'replica_3'=2,'tensor'=4]..., use_global_device_ids=true, to_apply=%region_12.13 | all-reduce | flops 1 | bytes 8 | tf_op jit(solution)/shard_map/psum | solution.py:60
  298.7 3.0 copy.206
  301.6 8.7 %psum.36 = f32[]{:T(128)} all-reduce(f32[]{:T(128)} %psum.35), channel_id=1, replica_groups=mesh['replica_0'=2,'replica_1'=4,'replica_2'=4,'replica_3'=2,'tensor'=4]..., use_global_device_ids=true, to_apply=%region_13.14 | all-reduce | flops 1 | bytes 8 | tf_op jit(solution)/shard_map/psum | solution.py:60
  310.3 7.9 %psum.37 = f32[]{:T(128)} all-reduce(f32[]{:T(128)} %psum.36), channel_id=1, replica_groups=mesh['replica_0'=2,'replica_1'=4,'replica_2'=4,'replica_3'=2,'tensor'=4]..., use_global_device_ids=true, to_apply=%region_14.15 | all-reduce | flops 1 | bytes 8 | tf_op jit(solution)/shard_map/psum | solution.py:60
  318.2 9.5 %psum.38 = f32[]{:T(128)} all-reduce(f32[]{:T(128)} %psum.37), channel_id=1, replica_groups=mesh['replica_0'=2,'replica_1'=4,'replica_2'=4,'replica_3'=2,'tensor'=4]..., use_global_device_ids=true, to_apply=%region_15.16 | all-reduce | flops 1 | bytes 8 | tf_op jit(solution)/shard_map/psum | solution.py:60
  327.7 4.0 reshape.117
  331.7 9.0 %psum.39 = f32[]{:T(128)} all-reduce(f32[]{:T(128)} %psum.38), channel_id=1, replica_groups=mesh['replica_0'=2,'replica_1'=4,'replica_2'=4,'replica_3'=2,'tensor'=4]..., use_global_device_ids=true, to_apply=%region_16.17 | all-reduce | flops 1 | bytes 8 | tf_op jit(solution)/shard_map/psum | solution.py:60
  343.7 4.9 %all-to-all-start.4 = ((bf16[32,32,1024]{2,1,0:T(8,128)(2,1)}), bf16[32,32,1024]{2,1,0:T(8,128)(2,1)}, u32[]{:S(2)}, u32[]{:S(2)}) async-start(bf16[32,32,1024]{2,1,0:T(8,128)(2,1)} %broadcast_in_dim.70), calls=%async_computation.4 | async-start | bytes 4194304 | tf_op jit(solution)/shard_map/all_to_all | solution.py:34
  348.6 6.5 %fusion.32 = f32[512,1024]{1,0:T(8,128)} fusion(bf16[512,2048]{1,0:T(8,128)(2,1)} %bitcast.143, bf16[1,2048,1024]{2,1,0:T(8,128)(2,1)} %param.26, f32[1024]{0:T(1024)S(1)} %copy-done.23), kind=kOutput, calls=%fused_computation.54 | convolution fusion | flops 2148007936 | bytes 8392704 | tf_op jit(solution)/shard_map/dot_general | solution.py:143
  355.1 4.5 %reshape.127 = f32[2,256,2,8,64]{4,3,2,1,0:T(8,128)} reshape(f32[512,1024]{1,0:T(8,128)} %fusion.32) | data formatting | bytes 4194304 | tf_op jit(solution)/shard_map/transpose(jvp())/reshape | solution.py:107
  359.6 2.9 copy.237
  362.5 4.5 %copy.212 = f32[2,256,2,8,64]{1,4,3,2,0:T(8,128)} copy(f32[2,256,2,8,64]{4,3,2,1,0:T(8,128)} %reshape.127) | data formatting | bytes 4194304 | tf_op jit(solution)/shard_map/transpose(jvp())/reshape | solution.py:107
  367.1 3.6 multiply_reduce_fusion
  374.1 4.0 %fusion.1 = f32[2,2,8,64,256]{4,3,2,1,0:T(8,128)} fusion(f32[2,2,8,256]{3,2,1,0:T(8,128)S(1)} %copy-done.22, f32[2,2,8,256]{3,2,1,0:T(8,128)S(1)} %copy-done.20, f32[2,2,256,256]{3,2,1,0:T(8,128)S(1)} %copy-done.14, pred[256,256]{1,0:T(8,128)(4,1)S(1)} %iota_compare_fusion, f32[2,256,2,8,64]{1,4,3,2,0:T(8,128)S(1)} %fusion.24), kind=kOutput, calls=%fused_computation.11 | convolution fusion | flops 278921216 | bytes 5373952 | tf_op jit(solution)/shard_map/transpose(jvp(cgrls,csgrp->clgrp))/dot_general | solution.py:88
  378.2 2.7 while.33
  390.4 9.1 %all_to_all.31 = bf16[2,32,32,1024]{3,2,1,0:T(8,128)(2,1)S(1)} all-to-all(bf16[2,32,32,1024]{3,2,1,0:T(8,128)(2,1)S(1)} %broadcast_in_dim.71), channel_id=1, replica_groups=mesh['replica_0'=2,'replica_1'=4,'replica_2'=4,'replica_3'=2,'tensor'=4]..., dimensions={0} | all-to-all | bytes 8388608 | tf_op jit(solution)/shard_map/all_to_all | solution.py:34
  399.5 2.5 copy.221
  (120 shorter events, 48.0 us)
Async XLA Ops:
  0.6 8.1 %copy-start.7 = (bf16[512,1024]{1,0:T(8,128)(2,1)S(1)}, bf16[512,1024]{1,0:T(8,128)(2,1)}, u32[]{:S(2)}) copy-start(bf16[512,1024]{1,0:T(8,128)(2,1)} %param.18) | copy-start | bytes 3145732
  8.7 13.9 %copy-start.9 = (bf16[2,256,2,128]{3,2,1,0:T(2,128)(2,1)}, bf16[2,256,2,128]{3,2,1,0:T(2,128)(2,1)S(1)}, u32[]{:S(2)}) copy-start(bf16[2,256,2,128]{3,2,1,0:T(2,128)(2,1)S(1)} %reshape.107) | copy-start | bytes 786436
  12.5 6.4 %copy-start.2 = (f32[512,1024]{0,1:T(8,128)}, f32[512,1024]{0,1:T(8,128)S(1)}, u32[]{:S(2)}) copy-start(f32[512,1024]{0,1:T(8,128)S(1)} %copy.208) | copy-start | bytes 6291460
  18.9 3.6 copy-start.26
  26.4 1.9 copy-start.10
  26.4 3.5 copy-start.6
  28.3 1.7 copy-start.4
  28.3 1.7 copy-start.19
  28.3 1.7 copy-start.21
  40.8 4.9 %copy-start.8 = (bf16[512,1024]{1,0:T(8,128)(2,1)S(1)}, bf16[512,1024]{1,0:T(8,128)(2,1)}, u32[]{:S(2)}) copy-start(bf16[512,1024]{1,0:T(8,128)(2,1)} %param.18) | copy-start | bytes 3145732
  45.8 3.5 copy-start.24
  48.9 2.7 copy-start.15
  157.2 43.1 %copy-start.25 = (bf16[1,2048,1024]{2,1,0:T(8,128)(2,1)S(1)}, bf16[1,2048,1024]{2,1,0:T(8,128)(2,1)}, u32[]{:S(2)}) copy-start(bf16[1,2048,1024]{2,1,0:T(8,128)(2,1)} %param.26) | copy-start | bytes 12582916
  157.5 42.8 %copy-start.16 = (bf16[512,1024]{1,0:T(8,128)(2,1)S(1)}, bf16[512,1024]{1,0:T(8,128)(2,1)}, u32[]{:S(2)}) copy-start(bf16[512,1024]{1,0:T(8,128)(2,1)} %copy-done.15) | copy-start | bytes 3145732
  200.3 2.5 copy-start.12
  291.2 2.5 copy-start.17
  327.7 13.7 %copy-start.18 = (f32[32,1024]{1,0:T(8,128)S(1)}, f32[32,1024]{1,0:T(8,128)}, u32[]{:S(2)}) copy-start(f32[32,1024]{1,0:T(8,128)} %param.28) | copy-start | bytes 393220
  343.7 4.9 %copy-start.23 = (f32[1024]{0:T(1024)S(1)}, f32[1024]{0:T(1024)}, u32[]{:S(2)}) copy-start(f32[1024]{0:T(1024)} %param.25) | copy-start | bytes 12292
  343.7 44.6 %all-to-all-start.4 = ((bf16[32,32,1024]{2,1,0:T(8,128)(2,1)}), bf16[32,32,1024]{2,1,0:T(8,128)(2,1)}, u32[]{:S(2)}, u32[]{:S(2)}) async-start(bf16[32,32,1024]{2,1,0:T(8,128)(2,1)} %broadcast_in_dim.70), calls=%async_computation.4 | async-start | bytes 4194304 | tf_op jit(solution)/shard_map/all_to_all | solution.py:34
  367.1 3.6 copy-start.3
  367.1 4.1 %copy-start.5 = (f32[2,256,2,8,64]{1,0,4,3,2:T(2,128)S(1)}, f32[2,256,2,8,64]{1,0,4,3,2:T(2,128)}, u32[]{:S(2)}) copy-start(f32[2,256,2,8,64]{1,0,4,3,2:T(2,128)} %reshape.114) | copy-start | bytes 6291460
  371.1 0.9 copy-start.11
  372.1 6.0 %copy-start = (f32[2,256,2,8,64]{1,4,3,2,0:T(8,128)}, f32[2,256,2,8,64]{1,4,3,2,0:T(8,128)S(1)}, u32[]{:S(2)}) copy-start(f32[2,256,2,8,64]{1,4,3,2,0:T(8,128)S(1)} %fusion.24) | copy-start | bytes 6291460
  372.1 2.0 copy-start.14
  372.1 2.0 copy-start.20
  372.1 2.0 copy-start.22
  378.2 3.5 copy-start.1
  380.9 0.8 copy-start.13
where the time goes:
time: 403 us; the launch traced here: 402 us
  blocking collectives  273 us (68%)
  local copies, waits for them, and re-layouts  61.2 us (15%)
  other arithmetic  32.8 us (8%)
  matrix products  27.9 us (7%)
  starting transfers between devices  4.89 us (1%)
    all_to_all x2, blocking collectives, sum_at_owner(): lax.all_to_all(split_up(value, dim, length), axis, 0, 0, tiled=True)  119 us
    all_to_all x1, blocking collectives, summed_rows(): lax.all_to_all(nearer, far, split_axis=0, concat_axis=0, tiled=True)  62.3 us
    all_to_all x2, blocking collectives, from_everyone(): lax.all_to_all(jnp.broadcast_to(value[None], (length, *value.shape)), axi...  51.9 us
    psum x5, blocking collectives, by_axis(): value = lax.psum(value, axis)  39.5 us
    reshape x3, local copies, waits for them, and re-layouts, gated_ssd(): ssd_out.reshape(tokens, group_count, width)  12.7 us
    reshape x3, local copies, waits for them, and re-layouts, gated_ssd(): (gated_vals * inv_norm).reshape(tokens, head_count * HEAD_DIM) * norm_gain  11.9 us
    reduce_sum x2, other arithmetic, sum_at_owner(): return jnp.sum(pieces, axis=0)  9.34 us
    unnamed x57, local copies, waits for them, and re-layouts  8.59 us
  transfers between devices with their start and end apart: 1, of which 0 were waited for; matrix products, arithmetic and copies ran while one was open for 9% of the time, Pallas kernels for 0%

commit v1 on v0

--- a/solution.py
+++ b/solution.py
@@ -1,6 +1,8 @@
 import jax
 import jax.numpy as jnp
 from jax import lax
+from jax.experimental import pallas as pl
+from jax.experimental.pallas import tpu as pltpu
 from jax.sharding import Mesh
 from jax.sharding import PartitionSpec as P
 
@@ -15,56 +17,383 @@
 outer_rate = 0.7
 outer_beta = 0.9
 clip_rms = 0.005
-
-
-def split_up(value, dim, length):
-    shape = value.shape
-    pieces = value.reshape(*shape[:dim], length, shape[dim] // length, *shape[dim + 1 :])
-    return jnp.moveaxis(pieces, dim, 0)
-
-
-def sum_at_owner(value, axis, dim):
-    length = lax.axis_size(axis)
-    pieces = lax.all_to_all(split_up(value, dim, length), axis, 0, 0, tiled=True)
-    return jnp.sum(pieces, axis=0)
-
-
-def from_everyone(value, axis):
-    length = lax.axis_size(axis)
-    return lax.all_to_all(
-        jnp.broadcast_to(value[None], (length, *value.shape)), axis, 0, 0, tiled=True
-    )
-
-
-def in_order(pieces, dim):
-    shape = list(pieces.shape[1:])
-    shape[dim] *= pieces.shape[0]
-    return jnp.moveaxis(pieces, 0, dim).reshape(shape)
-
-
-def gather_directly(value, axis, dim):
-    pieces = from_everyone(value, axis)
-    return in_order(pieces, dim)
-
-
-def summed_rows(value, axes, dim):
-    far, near = axes
-    pieces = split_up(value, dim, lax.axis_size(far))
-    nearer = sum_at_owner(pieces, near, dim + 1)
-    arrived = lax.all_to_all(nearer, far, split_axis=0, concat_axis=0, tiled=True)
-    return arrived.sum(axis=0)
-
-
-def by_axis(value, axes):
-    for axis in axes:
-        value = lax.psum(value, axis)
-    return value
-
-
-def whole_of(value, axes, dim):
-    far, near = axes
-    pieces = from_everyone(from_everyone(value, far), near)
-    return in_order(pieces.swapaxes(0, 1).reshape(-1, *value.shape), dim)
+MESH = pl.DeviceIdType.MESH
+UNITS = 8
+FEATURES = 256
+TOKENS = 128
+WIDTH = 1024
+ENTRIES = 2048 * 4096
+KINDS = ("far", "near", "mid", "ahead", "behind", "relay")
+LAGS = (0, 3, 4, 5, 6, 7, 8)
+
+
+def exchange_kernel(
+    normed,
+    weight,
+    target,
+    global_own,
+    momentum_own,
+    d_normed,
+    full,
+    new_global,
+    new_momentum,
+    part,
+    s_far,
+    s_near,
+    s_mid,
+    r_far,
+    r_near,
+    r_mid,
+    cot,
+    fresh,
+    r_core,
+    s_core,
+    r_x,
+    s_x,
+    r_y,
+    s_y,
+    s_z,
+    r_z,
+    sq_a,
+    sq_b,
+    sq_c,
+    z_send,
+    z_recv,
+    core_send,
+    core_recv,
+    x_send,
+    x_recv,
+    y_send,
+    y_recv,
+    zl_send,
+    zl_recv,
+    a_send,
+    a_recv,
+    b_send,
+    b_recv,
+    c_send,
+    c_recv,
+    g_send,
+    g_recv,
+):
+    zl = lax.axis_index("replica_0")
+    y = lax.axis_index("replica_1")
+    x = lax.axis_index("replica_2")
+    c = lax.axis_index("replica_3")
+    j = lax.axis_index("tensor")
+
+    def on_z(kz, kj):
+        return {"replica_0": lax.rem(zl + kz, 2), "tensor": lax.rem(j + kj, 4)}
+
+    def on_x(kx, kc):
+        return {"replica_2": lax.rem(x + kx, 4), "replica_3": lax.rem(c + kc, 2)}
+
+    def on_y(ky):
+        return {"replica_1": lax.rem(y + ky, 4)}
+
+    z_peers = [(kz, kj) for kz in range(2) for kj in range(4) if kz + kj]
+    x_peers = [(kx, kc) for kx in range(4) for kc in range(2) if kx + kc]
+    barrier = pltpu.get_barrier_semaphore()
+    for kz, kj in z_peers:
+        pl.semaphore_signal(barrier, inc=1, device_id=on_z(kz, kj), device_id_type=MESH)
+    for kx, kc in x_peers:
+        pl.semaphore_signal(barrier, inc=1, device_id=on_x(kx, kc), device_id_type=MESH)
+    for ky in range(1, 4):
+        pl.semaphore_signal(barrier, inc=1, device_id=on_y(ky), device_id_type=MESH)
+    pl.semaphore_wait(barrier, len(z_peers) + len(x_peers) + 3)
+
+    def remote(src, dst, send_sem, recv_sem, device):
+        return pltpu.make_async_remote_copy(
+            src_ref=src,
+            dst_ref=dst,
+            send_sem=send_sem,
+            recv_sem=recv_sem,
+            device_id=device,
+            device_id_type=MESH,
+        )
+
+    def way(u):
+        return 1 - 2 * lax.rem(u, 2)
+
+    def shard(step):
+        return lax.rem(j + step + 4, 4)
+
+    def z_copy(kind, u):
+        d = way(u)
+        ahead = {"tensor": shard(d)}
+        behind = {"tensor": shard(-d)}
+        src, dst, device = {
+            "far": lambda: (s_far.at[u], r_far.at[u], behind),
+            "near": lambda: (s_near.at[u], r_near.at[u], ahead),
+            "mid": lambda: (s_mid.at[u], r_mid.at[u], behind),
+            "ahead": lambda: (cot.at[u, j], cot.at[u, j], ahead),
+            "behind": lambda: (cot.at[u, j], cot.at[u, j], behind),
+            "relay": lambda: (cot.at[u, shard(-d)], cot.at[u, shard(-d)], ahead),
+        }[kind]()
+        slot = KINDS.index(kind)
+        return remote(src, dst, z_send.at[u, slot], z_recv.at[u, slot], device)
+
+    def core_copy(u):
+        return remote(
+            fresh.at[u, :, 1 - c],
+            r_core.at[u],
+            core_send.at[u],
+            core_recv.at[u],
+            {"replica_3": 1 - c},
+        )
+
+    def x_copy(u, k):
+        there = lax.rem(x + k, 4)
+        return remote(
+            s_core.at[u, there],
+            r_x.at[u, k - 1],
+            x_send.at[u, k - 1],
+            x_recv.at[u, k - 1],
+            {"replica_2": there},
+        )
+
+    def y_copy(half, k):
+        there = lax.rem(y + k, 4)
+        return remote(
+            s_x.at[half * 4 + there],
+            r_y.at[half, k - 1],
+            y_send.at[half, k - 1],
+            y_recv.at[half, k - 1],
+            {"replica_1": there},
+        )
+
+    def rows_of(u):
+        return pl.ds(pl.multiple_of(u * FEATURES, FEATURES), FEATURES)
+
+    def begin(u):
+        d = way(u)
+        products = lax.dot_general(
+            normed[...],
+            weight[rows_of(u), :],
+            (((1,), (1,)), ((), ())),
+            preferred_element_type=jnp.float32,
+        )
+        part[u] = products.reshape(4, TOKENS, FEATURES)
+        s_far[u] = part[u, shard(2)].astype(jnp.bfloat16)
+        s_near[u] = part[u, shard(d)].astype(jnp.bfloat16)
+        z_copy("far", u).start()
+        z_copy("near", u).start()
+
+    def pass_on(u):
+        z_copy("far", u).wait_recv()
+        s_mid[u] = (r_far[u].astype(jnp.float32) + part[u, shard(-way(u))]).astype(jnp.bfloat16)
+        z_copy("mid", u).start()
+
+    def own(u):
+        z_copy("near", u).wait_recv()
+        z_copy("mid", u).wait_recv()
+        total = part[u, j] + r_near[u].astype(jnp.float32) + r_mid[u].astype(jnp.float32)
+        cot[u, j] = (total - target[:, rows_of(u)].astype(jnp.float32)).astype(jnp.bfloat16)
+        z_copy("ahead", u).start()
+        z_copy("behind", u).start()
+
+    def relay(u):
+        z_copy("ahead", u).wait_recv()
+        z_copy("relay", u).start()
+
+    def gradients(u):
+        z_copy("behind", u).wait_recv()
+        z_copy("relay", u).wait_recv()
+        whole = cot[u].reshape(4 * TOKENS, FEATURES)
+        for first in range(0, WIDTH, 512):
+            cols = slice(first, first + 512)
+            rows = weight[rows_of(u), cols]
+            grad = lax.dot_general(
+                whole,
+                normed[:, cols],
+                (((0,), (0,)), ((), ())),
+                preferred_element_type=jnp.float32,
+            )
+            moved = (rows.astype(jnp.float32) - inner_rate * grad).astype(jnp.bfloat16)
+            fresh[u, :, :, :, cols] = moved.reshape(4, 2, 32, 512)
+            d_normed[:, cols] += jnp.dot(whole, rows, preferred_element_type=jnp.float32)
+        core_copy(u).start()
+
+    def over_x(u):
+        core_copy(u).wait_recv()
+        for i in range(4):
+            both = fresh[u, i, c].astype(jnp.float32) + r_core[u, i].astype(jnp.float32)
+            s_core[u, i] = both.astype(jnp.bfloat16)
+        for k in range(1, 4):
+            x_copy(u, k).start()
+
+    def after_x(u):
+        total = s_core[u, x].astype(jnp.float32)
+        for k in range(1, 4):
+            x_copy(u, k).wait_recv()
+            total = total + r_x[u, k - 1].astype(jnp.float32)
+        s_x[u] = total.astype(jnp.bfloat16)
+
+    d_normed[...] = jnp.zeros_like(d_normed)
+    stages = list(zip((begin, pass_on, own, relay, gradients, over_x, after_x), LAGS))
+
+    @pl.loop(0, UNITS + LAGS[-1])
+    def _(k):
+        for stage, lag in stages:
+
+            @pl.when((k >= lag) & (k < UNITS + lag))
+            def _():
+                stage(k - lag)
+
+    for half in range(2):
+        for k in range(1, 4):
+            y_copy(half, k).start()
+    for half in range(2):
+        total = s_x[half * 4 + y].astype(jnp.float32)
+        for k in range(1, 4):
+            y_copy(half, k).wait_recv()
+            total = total + r_y[half, k - 1].astype(jnp.float32)
+        s_y[half] = total
+    s_z[...] = s_y[1 - zl].astype(jnp.bfloat16)
+    over_z = remote(s_z, r_z, zl_send.at[0], zl_recv.at[0], on_z(1, 0))
+    over_z.start()
+    over_z.wait_recv()
+    delta = global_own[...] - (s_y[zl] + r_z[...].astype(jnp.float32)) * (1.0 / 64)
+
+    squares = jnp.sum((delta * delta).reshape(4, 8, WIDTH), axis=0)
+    folded = squares[:, :128]
+    for first in range(128, WIDTH, 128):
+        folded = folded + squares[:, first : first + 128]
+    sq_a[x, c] = folded
+    a_copies = [
+        remote(sq_a.at[x, c], sq_a.at[x, c], a_send.at[i], a_recv.at[i], on_x(*peer))
+        for i, peer in enumerate(x_peers)
+    ]
+    for copy in a_copies:
+        copy.start()
+    for copy in a_copies:
+        copy.wait_recv()
+    sq_b[y] = jnp.sum(sq_a[...].reshape(8, 8, 128), axis=0)
+    b_copies = [
+        remote(sq_b.at[y], sq_b.at[y], b_send.at[k - 1], b_recv.at[k - 1], on_y(k))
+        for k in range(1, 4)
+    ]
+    for copy in b_copies:
+        copy.start()
+    for copy in b_copies:
+        copy.wait_recv()
+    sq_c[zl, j] = jnp.sum(sq_b[...], axis=0)
+    c_copies = [
+        remote(sq_c.at[zl, j], sq_c.at[zl, j], c_send.at[i], c_recv.at[i], on_z(*peer))
+        for i, peer in enumerate(z_peers)
+    ]
+    for copy in c_copies:
+        copy.start()
+    for copy in c_copies:
+        copy.wait_recv()
+    square_sum = jnp.sum(jnp.sum(sq_c[...].reshape(8, 8, 128), axis=0), keepdims=True)
+    factor = jnp.minimum(1.0, clip_rms / jnp.sqrt(square_sum / ENTRIES + 1e-06))
+    clipped = factor * delta
+    moment = outer_beta * momentum_own[...] + clipped
+    moved = global_own[...] - outer_rate * (clipped + outer_beta * moment)
+    new_momentum[...] = moment
+    new_global[...] = moved
+    full[zl, y, x, c] = moved.astype(jnp.bfloat16)
+
+    def gather(index, src, device):
+        return remote(src, src, g_send.at[index], g_recv.at[index], device)
+
+    mine = full.at[zl, y, x, c]
+    first = gather(0, mine, on_z(1, 0))
+    first.start()
+    first.wait_recv()
+    left, right = pl.ds(0, WIDTH // 2), pl.ds(WIDTH // 2, WIDTH // 2)
+    near = [gather(k, full.at[:, y, x, c, :, left], on_y(k)) for k in range(1, 4)]
+    near += [gather(3 + k, full.at[:, y, x, c, :, right], on_x(k, 0)) for k in range(1, 4)]
+    for copy in near:
+        copy.start()
+    for copy in near:
+        copy.wait_recv()
+    far = [gather(6 + k, full.at[:, :, x, c, :, left], on_x(k, 0)) for k in range(1, 4)]
+    far += [gather(9 + k, full.at[:, y, :, c, :, right], on_y(k)) for k in range(1, 4)]
+    for i in (0, 3, 2, 5, 1, 4):
+        far[i].start()
+
+    def to_core(index, k):
+        if index < 4:
+            src = full.at[:, :, lax.rem(x + 4 - k, 4), c, :, left]
+        else:
+            src = full.at[:, lax.rem(y + 4 - k, 4), :, c, :, right]
+        return gather(13 + index, src, on_x(0, 1))
+
+    across = [to_core(0, 0), to_core(4, 0)]
+    for copy in across:
+        copy.start()
+    for k in (1, 3, 2):
+        for base in (0, 3):
+            far[base + k - 1].wait_recv()
+            copy = to_core(k if base == 0 else 4 + k, k)
+            copy.start()
+            across.append(copy)
+    for copy in across:
+        copy.wait_recv()
+
+    for copy in [over_z, first, *a_copies, *b_copies, *c_copies, *near, *far, *across]:
+        copy.wait_send()
+    for half in range(2):
+        for k in range(1, 4):
+            y_copy(half, k).wait_send()
+
+    @pl.loop(0, UNITS)
+    def _(u):
+        for kind in KINDS:
+            z_copy(kind, u).wait_send()
+        core_copy(u).wait_send()
+        for k in range(1, 4):
+            x_copy(u, k).wait_send()
+
+
+def exchange(normed, weight, target, global_own, momentum_own):
+    half = jnp.bfloat16
+    piece = (UNITS, TOKENS, FEATURES)
+    dma = pltpu.SemaphoreType.DMA
+    vmem = pl.BlockSpec(memory_space=pltpu.VMEM)
+    d_normed, full, new_global, new_momentum = pl.pallas_call(
+        exchange_kernel,
+        out_shape=(
+            jax.ShapeDtypeStruct((4 * TOKENS, WIDTH), jnp.float32),
+            jax.ShapeDtypeStruct((2, 4, 4, 2, 32, WIDTH), half),
+            jax.ShapeDtypeStruct((32, WIDTH), jnp.float32),
+            jax.ShapeDtypeStruct((32, WIDTH), jnp.float32),
+        ),
+        in_specs=[vmem] * 5,
+        out_specs=[vmem] * 4,
+        scratch_shapes=[
+            pltpu.VMEM((UNITS, 4, TOKENS, FEATURES), jnp.float32),
+            *[pltpu.VMEM(piece, half)] * 6,
+            pltpu.VMEM((UNITS, 4, TOKENS, FEATURES), half),
+            pltpu.VMEM((UNITS, 4, 2, 32, WIDTH), half),
+            pltpu.VMEM((UNITS, 4, 32, WIDTH), half),
+            pltpu.VMEM((UNITS, 4, 32, WIDTH), half),
+            pltpu.VMEM((UNITS, 3, 32, WIDTH), half),
+            pltpu.VMEM((UNITS, 32, WIDTH), half),
+            pltpu.VMEM((2, 3, 32, WIDTH), half),
+            pltpu.VMEM((2, 32, WIDTH), jnp.float32),
+            pltpu.VMEM((32, WIDTH), half),
+            pltpu.VMEM((32, WIDTH), half),
+            pltpu.VMEM((4, 2, 8, 128), jnp.float32),
+            pltpu.VMEM((4, 8, 128), jnp.float32),
+            pltpu.VMEM((2, 4, 8, 128), jnp.float32),
+            *[dma((UNITS, len(KINDS)))] * 2,
+            *[dma((UNITS,))] * 2,
+            *[dma((UNITS, 3))] * 2,
+            *[dma((2, 3))] * 2,
+            *[dma((1,))] * 2,
+            *[dma((7,))] * 2,
+            *[dma((3,))] * 2,
+            *[dma((7,))] * 2,
+            *[dma((21,))] * 2,
+        ],
+        compiler_params=pltpu.CompilerParams(
+            collective_id=0, has_side_effects=True, vmem_limit_bytes=60 * 2**20
+        ),
+    )(normed, weight, target, global_own, momentum_own)
+    return d_normed, full.reshape(2048, WIDTH), new_global, new_momentum
 
 
 def gated_ssd(inputs_f, gate_z, b_proj, c_proj, dt_raw, a_log, dt_bias, skip_d, norm_gain):
@@ -131,34 +460,10 @@
 
     normed_f, pull_back = jax.vjp(forward, x_in.astype(jnp.float32))
     normed = normed_f.astype(jnp.bfloat16)
-    layer_part = sum_at_owner(
-        lax.dot_general(
-            normed, local_weight, (((1,), (1,)), ((), ())), preferred_element_type=jnp.float32
-        ),
-        "tensor",
-        0,
-    )
-    cotangent_part = (layer_part - target.astype(jnp.float32)).astype(jnp.bfloat16)
-    cotangent = gather_directly(cotangent_part, "tensor", 0)
-    d_normed = jnp.dot(cotangent, local_weight, preferred_element_type=jnp.float32)
+    d_normed, new_weight, new_global, new_momentum = exchange(
+        normed, local_weight, target, global_weight, momentum
+    )
     grad_input = pull_back(d_normed)[0]
-    weight_grad = lax.dot_general(
-        cotangent, normed, (((0,), (0,)), ((), ())), preferred_element_type=jnp.float32
-    )
-    own_rows = local_weight.astype(jnp.float32)
-    whole_term = own_rows - inner_rate * weight_grad
-    summed = summed_rows(whole_term, (("replica_0", "replica_1", "replica_2"), "replica_3"), 0)
-    replicas = lax.axis_size(REPLICA)
-    delta = global_weight - summed / replicas
-    square_sum = by_axis(jnp.sum(delta * delta), REPLICA_TENSOR)
-    entry_count = delta.shape[0] * delta.shape[1] * replicas * lax.axis_size("tensor")
-    factor = jnp.minimum(1.0, clip_rms / jnp.sqrt(square_sum / entry_count + 1e-06))
-    clipped = factor * delta
-    new_momentum = outer_beta * momentum + clipped
-    new_global = global_weight - outer_rate * (clipped + outer_beta * new_momentum)
-    new_weight = whole_of(
-        new_global.astype(jnp.bfloat16), (("replica_0", "replica_1", "replica_2"), "replica_3"), 0
-    )
     return (grad_input.astype(jnp.bfloat16), new_weight, new_global, new_momentum)
 
 

time: 403 us -> 240 us (0.60)
  blocking collectives: 273 us -> 0 us
  Pallas kernels: 0 us -> 147 us
  other arithmetic: 32.8 us -> 21 us
  matrix products: 27.9 us -> 16.3 us
  local copies, waits for them, and re-layouts: 61.2 us -> 53.8 us
  starting transfers between devices: 4.89 us -> 0 us
    all_to_all x5 -> x0, blocking collectives: 234 us -> none  [the longest x2 119 us: sum_at_owner(): lax.all_to_all(split_up(value, dim, length), axis, 0, 0, tiled=True)]
    pallas_call x0 -> x1, Pallas kernels: none -> 147 us  [exchange(): pl.pallas_call(exchange_kernel, out_shape=(jax.ShapeDtypeStruct((4 * TOKE...]
    psum x5 -> x0, blocking collectives: 39.5 us -> none  [by_axis(): value = lax.psum(value, axis)]
    reduce_sum x4 -> x0, other arithmetic: 12.4 us -> none  [the longest x2 9.34 us: sum_at_owner(): return jnp.sum(pieces, axis=0)]
    dot_general x3 -> x0, matrix products: 11.4 us -> none  [the longest x1 6.49 us: shards(): jnp.dot(cotangent, local_weight, preferred_element_type=jnp.float32)]
    all_to_all x1 -> x0, starting transfers between devices: 4.89 us -> none  [from_everyone(): lax.all_to_all(jnp.broadcast_to(value[None], (length, *value.shape)), axi...]
    unnamed x57 -> x38, local copies, waits for them, and re-layouts: 8.59 us -> 13 us
  transfers between devices with their start and end apart: 1 -> 0, of which waited for: 0 -> 0; matrix products, arithmetic and copies ran while one was open for 9% -> 0% of each run, Pallas kernels for 0% -> 0%
where the time goes in v1:
time: 240 us
  Pallas kernels  147 us (61%)
  local copies, waits for them, and re-layouts  53.8 us (22%)
  other arithmetic  21 us (9%)
  matrix products  16.3 us (7%)
    pallas_call x1, Pallas kernels, exchange(): pl.pallas_call(exchange_kernel, out_shape=(jax.ShapeDtypeStruct((4 * TOKE...  147 us
    unnamed x38, local copies, waits for them, and re-layouts  13 us
    reshape x3, local copies, waits for them, and re-layouts, gated_ssd(): ssd_out.reshape(tokens, group_count, width)  12.6 us
    reshape x3, local copies, waits for them, and re-layouts, gated_ssd(): (gated_vals * inv_norm).reshape(tokens, head_count * HEAD_DIM) * norm_gain  12 us
    dot_general x2, matrix products, gated_ssd(): inside = jnp.einsum('cgrls,csgrp->clgrp', weights, values)  9.6 us

profile of v1, /device:TPU:1, one launch (start us, length us, event | category | flops | bytes accessed | tf_op | source)
XLA Modules:
  0.0 239.6 jit_solution(13921682351387826513)
XLA Ops:
  2.4 2.3 reduce-window.6
  5.3 1.0 reshape.103
  6.3 3.0 %reshape.123 = bf16[2,256,2,8,64]{4,3,2,1,0:T(8,128)(2,1)S(1)} reshape(bf16[512,1024]{1,0:T(8,128)(2,1)} %param.17) | data formatting | bytes 2097152 | tf_op jit(solution)/shard_map/jvp()/reshape | solution.py:405
  9.3 1.7 copy.101
  13.1 1.8 fusion.34
  14.9 1.3 fusion.30
  16.8 1.9 convert_multiply_fusion
  18.7 1.9 copy.108
  20.6 2.4 reshape.109
  23.8 5.7 %multiply_reduce_fusion.1 = (f32[2,256,2]{1,2,0:T(2,128)S(1)}, f32[2,256,2,8,64]{1,4,3,2,0:T(8,128)S(1)}) fusion(f32[2,256,2,8,64]{1,0,4,3,2:T(2,128)} %reshape.109, bf16[2,256,2,8,64]{1,4,3,2,0:T(8,128)(2,1)S(1)} %copy.101, f32[2,8]{1,0:T(2,128)S(1)} %mul.178, f32[2,256,2,8]{1,3,2,0:T(8,128)S(1)} %get-tuple-element.224, f32[2,2,8,64,256]{4,3,2,1,0:T(8,128)} %fusion.34, ...), kind=kOutput, calls=%fused_computation.46 | convolution fusion | flops 283114496 | bytes 8556608 | tf_op jit(solution)/shard_map/jvp(cgrls,csgrp->clgrp)/dot_general | solution.py:417
  29.5 3.8 %copy.131 = f32[2,256,2,8,64]{4,3,2,1,0:T(8,128)} copy(f32[2,256,2,8,64]{1,4,3,2,0:T(8,128)S(1)} %get-tuple-element.229) | data formatting | bytes 4194304 | tf_op jit(solution)/shard_map/jvp()/reshape | solution.py:432
  33.3 4.9 %reshape.120 = f32[512,1024]{1,0:T(8,128)} reshape(f32[2,256,2,8,64]{4,3,2,1,0:T(8,128)} %copy.131) | data formatting | bytes 4194304 | tf_op jit(solution)/shard_map/jvp()/reshape | solution.py:432
  39.5 1.1 copy-done.3
  40.9 1.8 multiply_convert_fusion.normed
  42.7 147.3 %shard_map.156 = (f32[512,1024]{1,0:T(8,128)}, bf16[2,4,4,2,32,1024]{5,4,3,2,1,0:T(8,128)(2,1)}, f32[32,1024]{1,0:T(8,128)}, f32[32,1024]{1,0:T(8,128)}) custom-call(bf16[512,1024]{1,0:T(8,128)(2,1)} %multiply_convert_fusion.normed, bf16[2048,1024]{1,0:T(8,128)(2,1)} %bitcast.117, bf16[128,2048]{1,0:T(8,128)(2,1)} %target.1, f32[32,1024]{1,0:T(8,128)} %global_own.1, ...), custom_call_target="tpu_custom_call" | custom-call | tf_op jit(solution)/shard_map/pallas_call | solution.py:356
  190.0 3.3 %broadcast_multiply_fusion = f32[512,1024]{1,0:T(8,128)} fusion(f32[512,1024]{1,0:T(8,128)} %get-tuple-element.145, f32[1024]{0:T(1024)S(1)} %copy-done.14), kind=kLoop, calls=%fused_computation.48 | loop fusion | flops 524288 | bytes 4198400 | tf_op jit(solution)/shard_map/transpose(jvp())/mul | solution.py:436
  193.3 2.9 %copy.135 = f32[512,1024]{0,1:T(8,128)} copy(f32[512,1024]{1,0:T(8,128)} %broadcast_multiply_fusion) | data formatting | bytes 4194304 | tf_op jit(solution)/shard_map/transpose(jvp())/reshape | solution.py:436
  196.2 3.0 %copy.106 = f32[2,256,2,8,64]{1,0,4,3,2:T(2,128)} copy(f32[2,256,2,8,64]{1,4,3,2,0:T(8,128)S(1)} %get-tuple-element.229) | data formatting | bytes 4194304 | tf_op jit(solution)/shard_map/jvp()/add | solution.py:430
  199.2 3.9 %reshape.111 = f32[512,2,512]{0,2,1:T(8,128)} reshape(f32[2,256,2,8,64]{1,0,4,3,2:T(2,128)} %copy.106) | data formatting | bytes 4194304 | tf_op jit(solution)/shard_map/jvp()/reshape | solution.py:432
  203.1 3.4 %multiply_reduce_fusion = f32[512,2]{0,1:T(2,128)S(1)} fusion(f32[512,2,512]{0,2,1:T(8,128)} %reshape.111, f32[512,1024]{0,1:T(8,128)} %copy.135, f32[512,1024]{0,1:T(8,128)} %copy-done.2), kind=kLoop, calls=%fused_computation.44 | loop fusion | flops 1571840 | bytes 6295552 | tf_op jit(solution)/shard_map/transpose(jvp())/reduce_sum | solution.py:436
  206.5 4.5 %reshape.121 = f32[2,256,2,8,64]{4,3,2,1,0:T(8,128)} reshape(f32[512,1024]{1,0:T(8,128)} %broadcast_multiply_fusion) | data formatting | bytes 4194304 | tf_op jit(solution)/shard_map/transpose(jvp())/reshape | solution.py:436
  211.0 4.6 %copy.112 = f32[2,256,2,8,64]{1,4,3,2,0:T(8,128)} copy(f32[2,256,2,8,64]{4,3,2,1,0:T(8,128)} %reshape.121) | data formatting | bytes 4194304 | tf_op jit(solution)/shard_map/transpose(jvp())/reshape | solution.py:436
  215.6 2.9 %fusion.20 = f32[2,256,2,8,64]{1,4,3,2,0:T(8,128)S(1)} fusion(f32[2,256,2,8,64]{1,4,3,2,0:T(8,128)} %copy.112, f32[2,256,2,8,64]{1,0,4,3,2:T(2,128)} %reshape.109, f32[2,256,2,8,64]{1,4,3,2,0:T(8,128)S(1)} %get-tuple-element.229, f32[2,256,2]{1,2,0:T(2,128)S(1)} %multiply_multiply_fusion.5, f32[2,256,2]{1,2,0:T(2,128)S(1)} %fusion.38), kind=kLoop, calls=%fused_computation.33 | loop fusion | flops 3145728 | bytes 8396800 | tf_op jit(solution)/shard_map/transpose(jvp())/mul | solution.py:432
  218.5 1.6 fusion.24
  220.3 2.7 %while.33 = (s32[]{:T(128)}, f32[2,8,64,128]{3,2,1,0:T(8,128)S(1)}, bf16[2,2,8,64,128]{4,3,2,1,0:T(8,128)(2,1)S(1)}, f32[2,2,8,64,128]{4,3,2,1,0:T(8,128)}, f32[...) while((s32[]{:T(128)}, f32[2,8,64,128]{3,2,1,0:T(8,128)S(1)}, ...), condition=%wide.region_7.8_spmd.clone, body=%wide.region_6.7_spmd.clone.sunk | while | flops 524292 | bytes 2359600 | solution.py:426
  220.4 1.3 bitcast_add_fusion.6
  221.8 1.2 bitcast_add_fusion.6
  223.8 3.9 %fusion.1 = f32[2,2,8,64,256]{4,3,2,1,0:T(8,128)S(1)} fusion(f32[2,2,8,256]{3,2,1,0:T(8,128)} %copy.99, f32[2,2,8,256]{3,2,1,0:T(8,128)} %copy-done.12, f32[2,2,256,256]{3,2,1,0:T(8,128)} %fusion.30, pred[256,256]{1,0:T(8,128)(4,1)S(1)} %copy-done.11, f32[2,256,2,8,64]{1,4,3,2,0:T(8,128)S(1)} %copy-done.1), kind=kOutput, calls=%fused_computation.9 | convolution fusion | flops 278921216 | bytes 5373952 | tf_op jit(solution)/shard_map/transpose(jvp(cgrls,csgrp->clgrp))/dot_general | solution.py:417
  227.7 1.6 fusion.21
  229.3 2.0 copy.140
  231.3 2.3 reshape.122
  233.6 4.7 %copy.201 = bf16[2048,1024]{1,0:T(8,128)(2,1)} copy(bf16[2048,1024]{1,0:T(8,128)(2,1)} %bitcast.118) | data formatting | bytes 8388608
  (77 shorter events, 10.3 us)
Async XLA Ops:
  5.0 18.8 %copy-start.12 = (f32[2,2,8,256]{3,2,1,0:T(8,128)}, f32[2,2,8,256]{3,2,1,0:T(8,128)S(1)}, u32[]{:S(2)}) copy-start(f32[2,2,8,256]{3,2,1,0:T(8,128)S(1)} %get-tuple-element.227) | copy-start | bytes 98308
  13.1 3.1 %copy-start.6 = (bf16[2,256,2,128]{3,2,1,0:T(2,128)(2,1)}, bf16[2,256,2,128]{3,2,1,0:T(2,128)(2,1)S(1)}, u32[]{:S(2)}) copy-start(bf16[2,256,2,128]{3,2,1,0:T(2,128)(2,1)S(1)} %reshape.102) | copy-start | bytes 786436
  13.1 3.7 %copy-start.4 = (bf16[512,1024]{1,0:T(8,128)(2,1)S(1)}, bf16[512,1024]{1,0:T(8,128)(2,1)}, u32[]{:S(2)}) copy-start(bf16[512,1024]{1,0:T(8,128)(2,1)} %param.18) | copy-start | bytes 3145732
  20.6 2.4 %copy-start.2 = (f32[512,1024]{0,1:T(8,128)}, f32[512,1024]{0,1:T(8,128)S(1)}, u32[]{:S(2)}) copy-start(f32[512,1024]{0,1:T(8,128)S(1)} %copy.108) | copy-start | bytes 6291460
  20.6 3.1 %copy-start.15 = (f32[16]{0:T(128)S(1)}, f32[16]{0:T(128)}, u32[]{:S(2)}) copy-start(f32[16]{0:T(128)} %param.24) | copy-start | bytes 196
  20.6 3.2 %copy-start.13 = (f32[2,2,8,256]{3,2,1,0:T(8,128)S(1)}, f32[2,2,8,256]{3,2,1,0:T(8,128)}, u32[]{:S(2)}) copy-start(f32[2,2,8,256]{3,2,1,0:T(8,128)} %copy.99) | copy-start | bytes 98308
  39.0 1.6 copy-start.3
  39.0 1.8 copy-start.5
  39.0 1.8 copy-start.14
  215.6 2.9 %copy-start.7 = (bf16[2,256,2,128]{3,2,1,0:T(2,128)(2,1)S(1)}, bf16[2,256,2,128]{3,2,1,0:T(2,128)(2,1)}, u32[]{:S(2)}) copy-start(bf16[2,256,2,128]{3,2,1,0:T(2,128)(2,1)} %copy-done.6) | copy-start | bytes 786436
  218.5 1.7 copy-start
  220.2 3.5 %copy-start.1 = (f32[2,256,2,8,64]{1,4,3,2,0:T(8,128)S(1)}, f32[2,256,2,8,64]{1,4,3,2,0:T(8,128)}, u32[]{:S(2)}) copy-start(f32[2,256,2,8,64]{1,4,3,2,0:T(8,128)} %copy-done) | copy-start | bytes 6291460
  220.3 3.5 %copy-start.11 = (pred[256,256]{1,0:T(8,128)(4,1)S(1)}, pred[256,256]{1,0:T(8,128)(4,1)}, u32[]{:S(2)}) copy-start(pred[256,256]{1,0:T(8,128)(4,1)} %iota_compare_fusion) | copy-start | bytes 196612
  223.0 0.8 copy-start.8
  233.6 4.7 %copy-start.10 = (f32[32,1024]{1,0:T(8,128)S(1)}, f32[32,1024]{1,0:T(8,128)}, u32[]{:S(2)}) copy-start(f32[32,1024]{1,0:T(8,128)} %get-tuple-element.349) | copy-start | bytes 393220
  233.6 5.3 %copy-start.9 = (f32[32,1024]{1,0:T(8,128)S(1)}, f32[32,1024]{1,0:T(8,128)}, u32[]{:S(2)}) copy-start(f32[32,1024]{1,0:T(8,128)} %get-tuple-element.350) | copy-start | bytes 393220

commit v2 on v1

--- a/solution.py
+++ b/solution.py
@@ -396,44 +396,163 @@
     return d_normed, full.reshape(2048, WIDTH), new_global, new_momentum
 
 
-def gated_ssd(inputs_f, gate_z, b_proj, c_proj, dt_raw, a_log, dt_bias, skip_d, norm_gain):
-    tokens = inputs_f.shape[0]
-    head_count = a_log.shape[0]
-    group_count = b_proj.shape[1] // STATE
-    per_group = head_count // group_count
-    block_count = tokens // SPAN
-    values = inputs_f.reshape(block_count, SPAN, group_count, per_group, HEAD_DIM)
-    step_size = jax.nn.softplus(dt_raw + dt_bias).reshape(block_count, SPAN, group_count, per_group)
-    log_decay = (-jnp.exp(a_log)).reshape(group_count, per_group) * step_size
-    cum_decay = jnp.cumsum(log_decay, axis=1)
-    key_proj = b_proj.astype(jnp.float32).reshape(block_count, SPAN, group_count, STATE)
-    query_proj = c_proj.astype(jnp.float32).reshape(block_count, SPAN, group_count, STATE)
-    scores = jnp.einsum("clgn,csgn->cgls", query_proj, key_proj)
-    cumulative = cum_decay.transpose(0, 2, 3, 1)
-    gap_decay = cumulative[..., :, None] - cumulative[..., None, :]
-    causal_mask = jnp.tril(jnp.ones((SPAN, SPAN), dtype=bool))
-    decay_table = jnp.where(causal_mask, jnp.exp(jnp.where(causal_mask, gap_decay, 0.0)), 0.0)
-    weights = scores[:, :, None] * decay_table * step_size.transpose(0, 2, 3, 1)[..., None, :]
-    inside = jnp.einsum("cgrls,csgrp->clgrp", weights, values)
-    tail_weight = jnp.exp(cum_decay[:, -1:] - cum_decay) * step_size
-    states = jnp.einsum("csgn,csgr,csgrp->cgrpn", key_proj, tail_weight, values)
-    span_fade = jnp.exp(cum_decay[:, -1])
-
-    def carry_state(carried, inputs_pair):
-        fade_now, state_now = inputs_pair
-        return (fade_now[..., None, None] * carried + state_now, carried)
-
-    _, entering = lax.scan(
-        carry_state, jnp.zeros(states.shape[1:], jnp.float32), (span_fade, states)
-    )
-    outside = jnp.einsum("clgn,cgrpn->clgrp", query_proj, entering) * jnp.exp(cum_decay)[..., None]
-    ssd_out = inside + outside + skip_d.reshape(group_count, per_group)[..., None] * values
-    width = per_group * HEAD_DIM
-    gated_vals = ssd_out.reshape(tokens, group_count, width) * jax.nn.silu(
-        gate_z.astype(jnp.float32)
-    ).reshape(tokens, group_count, width)
-    inv_norm = lax.rsqrt(jnp.mean(gated_vals * gated_vals, axis=-1, keepdims=True) + 1e-05)
-    return (gated_vals * inv_norm).reshape(tokens, head_count * HEAD_DIM) * norm_gain
+def head_scalars(ref, first, tokens):
+    row = lax.broadcasted_iota(jnp.int32, (8, tokens), 0)
+    out = jnp.zeros((8, tokens), jnp.float32)
+    for r in range(8):
+        out = jnp.where(row == r, ref[first + r], out)
+    return out
+
+
+def dot(a, b, over, **settings):
+    return lax.dot_general(
+        a, b, ((over[:1], over[1:]), ((), ())), preferred_element_type=jnp.float32, **settings
+    )
+
+
+def decays(dt, a_log, dt_bias, first):
+    tokens = dt.shape[1]
+    raw = dt[...] + head_scalars(dt_bias, first, tokens)
+    step = jnp.maximum(raw, 0.0) + jnp.log1p(jnp.exp(-jnp.abs(raw)))
+    rate = -jnp.exp(head_scalars(a_log, first, tokens)) * step
+    below = lax.broadcasted_iota(jnp.int32, (SPAN, SPAN), 0) >= lax.broadcasted_iota(
+        jnp.int32, (SPAN, SPAN), 1
+    )
+    ones = jnp.where(below, 1.0, 0.0)
+    steps, by_row, by_column = [], [], []
+    for k in range(2):
+        own = rate[:, k * SPAN : (k + 1) * SPAN]
+        steps.append(step[:, k * SPAN : (k + 1) * SPAN])
+        by_row.append(dot(own, ones, (1, 1), precision=lax.Precision.HIGHEST))
+        by_column.append(dot(ones, own, (1, 1), precision=lax.Precision.HIGHEST))
+    return below, steps, by_row, by_column
+
+
+def tail_keys(keys, step, cum):
+    weight = jnp.exp(cum[:, SPAN - 1 :] - cum) * step
+    turned = keys.astype(jnp.float32).T
+    return [(turned * weight[r : r + 1]).astype(jnp.bfloat16) for r in range(8)]
+
+
+def paired(low, one, two):
+    return jnp.where(low, one, two)
+
+
+def forward_kernel(
+    a_log, dt_bias, skip, x_ref, z_ref, b_ref, c_ref, dt_ref, gain_ref, normed_ref, gated_ref, w_ref
+):
+    first = pl.program_id(0) * 8
+    below, steps, by_row, by_column = decays(dt_ref, a_log, dt_bias, first)
+    low = lax.broadcasted_iota(jnp.int32, (1, 128), 1) < HEAD_DIM
+    tails = tail_keys(b_ref[:SPAN], steps[0], by_row[0])
+    for k in range(2):
+        rows = slice(k * SPAN, (k + 1) * SPAN)
+        scores = dot(c_ref[rows], b_ref[rows], (1, 1))
+        squares = jnp.zeros((SPAN, 1), jnp.float32)
+        for q in range(4):
+            cols = slice(q * 128, (q + 1) * 128)
+            values = x_ref[rows, cols]
+            sides = []
+            for r in (2 * q, 2 * q + 1):
+                gap = by_column[k][:, r : r + 1] - by_row[k][r : r + 1]
+                table = jnp.where(below, jnp.exp(gap), 0.0)
+                weights = (scores * table * steps[k][r : r + 1]).astype(jnp.bfloat16)
+                w_ref[0, k, r] = weights
+                sides.append(dot(weights, values, (1, 0)))
+            skips = paired(low, skip[first + 2 * q], skip[first + 2 * q + 1])
+            out = paired(low, *sides) + skips * values.astype(jnp.float32)
+            if k == 1:
+                earlier = x_ref[:SPAN, cols]
+                state = paired(low, *[dot(tails[r], earlier, (1, 0)) for r in (2 * q, 2 * q + 1)])
+                fade = jnp.exp(
+                    paired(low, *[by_column[1][:, r : r + 1] for r in (2 * q, 2 * q + 1)])
+                )
+                out = out + dot(c_ref[rows], state.astype(jnp.bfloat16), (1, 0)) * fade
+            z = z_ref[rows, cols].astype(jnp.float32)
+            gated = out * (z / (1.0 + jnp.exp(-z)))
+            gated_ref[rows, cols] = gated
+            squares = squares + jnp.sum(gated * gated, axis=1, keepdims=True)
+        scale = lax.rsqrt(squares * (1.0 / 512) + 1e-05)
+        normed_ref[rows] = (gated_ref[rows] * scale * gain_ref[...]).astype(jnp.bfloat16)
+
+
+def backward_kernel(
+    a_log, dt_bias, skip, dn_ref, gated_ref, z_ref, w_ref, b_ref, c_ref, dt_ref, gain_ref, out_ref
+):
+    first = pl.program_id(0) * 8
+    _, steps, by_row, by_column = decays(dt_ref, a_log, dt_bias, first)
+    low = lax.broadcasted_iota(jnp.int32, (1, 128), 1) < HEAD_DIM
+    tails = tail_keys(b_ref[:SPAN], steps[0], by_row[0])
+    states = []
+    for k in (1, 0):
+        rows = slice(k * SPAN, (k + 1) * SPAN)
+        gated = gated_ref[rows]
+        pulled = dn_ref[rows] * gain_ref[...]
+        mean = jnp.sum(gated * gated, axis=1, keepdims=True) * (1.0 / 512)
+        scale = lax.rsqrt(mean + 1e-05)
+        along = jnp.sum(gated * pulled, axis=1, keepdims=True) * (1.0 / 512)
+        fall = along * scale * scale
+        for q in range(4):
+            cols = slice(q * 128, (q + 1) * 128)
+            z = z_ref[rows, cols].astype(jnp.float32)
+            own = dn_ref[rows, cols] * gain_ref[:, cols] - gated_ref[rows, cols] * fall
+            ssd = own * scale * (z / (1.0 + jnp.exp(-z)))
+            short = ssd.astype(jnp.bfloat16)
+            sides = [dot(w_ref[0, k, r], short, (0, 0)) for r in (2 * q, 2 * q + 1)]
+            skips = paired(low, skip[first + 2 * q], skip[first + 2 * q + 1])
+            grad = paired(low, *sides) + skips * ssd
+            if k == 1:
+                fade = jnp.exp(
+                    paired(low, *[by_column[1][:, r : r + 1] for r in (2 * q, 2 * q + 1)])
+                )
+                states.append(
+                    dot(c_ref[rows], (ssd * fade).astype(jnp.bfloat16), (0, 0)).astype(
+                        jnp.bfloat16
+                    )
+                )
+            else:
+                grad = grad + paired(
+                    low, *[dot(tails[r], states[q], (0, 0)) for r in (2 * q, 2 * q + 1)]
+                )
+            out_ref[rows, cols] = grad.astype(jnp.bfloat16)
+
+
+def group_specs():
+    small = pl.BlockSpec(memory_space=pltpu.SMEM)
+    wide = pl.BlockSpec((512, 512), lambda g: (0, g))
+    state = pl.BlockSpec((512, STATE), lambda g: (0, g))
+    heads = pl.BlockSpec((8, 512), lambda g: (g, 0))
+    gain = pl.BlockSpec((1, 512), lambda g: (0, g))
+    tables = pl.BlockSpec((1, 2, 8, SPAN, SPAN), lambda g: (g, 0, 0, 0, 0))
+    return small, wide, state, heads, gain, tables
+
+
+def forward(x_in, gate_z, b_proj, c_proj, dt, a_log, dt_bias, skip_d, gain_row):
+    small, wide, state, heads, gain, tables = group_specs()
+    return pl.pallas_call(
+        forward_kernel,
+        grid=(2,),
+        out_shape=(
+            jax.ShapeDtypeStruct((512, WIDTH), jnp.bfloat16),
+            jax.ShapeDtypeStruct((512, WIDTH), jnp.float32),
+            jax.ShapeDtypeStruct((2, 2, 8, SPAN, SPAN), jnp.bfloat16),
+        ),
+        in_specs=[small, small, small, wide, wide, state, state, heads, gain],
+        out_specs=[wide, wide, tables],
+        compiler_params=pltpu.CompilerParams(vmem_limit_bytes=48 * 2**20),
+    )(a_log, dt_bias, skip_d, x_in, gate_z, b_proj, c_proj, dt, gain_row)
+
+
+def pull_back(d_normed, gated, gate_z, tables_in, b_proj, c_proj, dt, a_log, dt_bias, skip_d, row):
+    small, wide, state, heads, gain, tables = group_specs()
+    return pl.pallas_call(
+        backward_kernel,
+        grid=(2,),
+        out_shape=jax.ShapeDtypeStruct((512, WIDTH), jnp.bfloat16),
+        in_specs=[small, small, small, wide, wide, wide, tables, state, state, heads, gain],
+        out_specs=wide,
+        compiler_params=pltpu.CompilerParams(vmem_limit_bytes=48 * 2**20),
+    )(a_log, dt_bias, skip_d, d_normed, gated, gate_z, tables_in, b_proj, c_proj, dt, row)
 
 
 def shards(
@@ -453,18 +572,18 @@
 ):
     local_weight = out_weight[0]
 
-    def forward(inputs_f):
-        return gated_ssd(
-            inputs_f, gate_z, b_proj, c_proj, dt_raw, a_log, dt_bias, skip_d, norm_gain
-        )
-
-    normed_f, pull_back = jax.vjp(forward, x_in.astype(jnp.float32))
-    normed = normed_f.astype(jnp.bfloat16)
+    dt = dt_raw.T
+    gain_row = norm_gain.reshape(1, WIDTH)
+    normed, gated, tables = forward(
+        x_in, gate_z, b_proj, c_proj, dt, a_log, dt_bias, skip_d, gain_row
+    )
     d_normed, new_weight, new_global, new_momentum = exchange(
         normed, local_weight, target, global_weight, momentum
     )
-    grad_input = pull_back(d_normed)[0]
-    return (grad_input.astype(jnp.bfloat16), new_weight, new_global, new_momentum)
+    grad_x = pull_back(
+        d_normed, gated, gate_z, tables, b_proj, c_proj, dt, a_log, dt_bias, skip_d, gain_row
+    )
+    return (grad_x, new_weight, new_global, new_momentum)
 
 
 def solution(mesh):

time: 240 us -> 177 us (0.74)
  local copies, waits for them, and re-layouts: 53.8 us -> 13.7 us
  other arithmetic: 21 us -> 0 us
  matrix products: 16.3 us -> 0 us
  Pallas kernels: 147 us -> 162 us
    reshape x14 -> x0, local copies, waits for them, and re-layouts: 33.7 us -> none  [the longest x3 12.6 us: gated_ssd(): ssd_out.reshape(tokens, group_count, width)]
    dot_general x7 -> x0, matrix products: 16.3 us -> none  [the longest x2 9.6 us: gated_ssd(): inside = jnp.einsum('cgrls,csgrp->clgrp', weights, values)]
    pallas_call x0 -> x2, Pallas kernels: none -> 14.8 us  [the longest x1 8.4 us: forward(): pl.pallas_call(forward_kernel, grid=(2,), out_shape=(jax.ShapeDtypeStruct...]
    mul x3 -> x0, other arithmetic: 8.04 us -> none  [the longest x1 3.31 us: gated_ssd(): (gated_vals * inv_norm).reshape(tokens, head_count * HEAD_DIM) * norm_gain]
    reduce_sum x1 -> x0, other arithmetic: 3.39 us -> none  [gated_ssd(): gated_vals * inv_norm]
    add x1 -> x0, local copies, waits for them, and re-layouts: 2.96 us -> none  [gated_ssd(): inside + outside]
    mul x8 -> x0, local copies, waits for them, and re-layouts: 2.84 us -> none  [the longest x1 1.92 us: gated_ssd(): jax.nn.silu(gate_z.astype(jnp.float32)).reshape(tokens, group_count, width)]
    add_any x2 -> x0, other arithmetic: 2.45 us -> none  [carry_state(): return (fade_now[..., None, None] * carried + state_now, carried)]
where the time goes in v2:
time: 177 us
  Pallas kernels  162 us (92%)
  local copies, waits for them, and re-layouts  13.7 us (8%)
    pallas_call x1, Pallas kernels, exchange(): pl.pallas_call(exchange_kernel, out_shape=(jax.ShapeDtypeStruct((4 * TOKE...  147 us
    unnamed x47, local copies, waits for them, and re-layouts  13.7 us
    pallas_call x1, Pallas kernels, forward(): pl.pallas_call(forward_kernel, grid=(2,), out_shape=(jax.ShapeDtypeStruct...  8.4 us
    pallas_call x1, Pallas kernels, pull_back(): pl.pallas_call(backward_kernel, grid=(2,), out_shape=jax.ShapeDtypeStruct...  6.42 us

profile of v2, /device:TPU:1, one launch (start us, length us, event | category | flops | bytes accessed | tf_op | source)
XLA Modules:
  0.0 176.7 jit_solution(5208872123671921077)
XLA Ops:
  0.6 0.0 copy-start
  0.6 1.2 copy-done
  1.9 1.2 copy-done.3
  3.1 0.9 copy-done.5
  4.0 0.9 copy-done.7
  5.0 0.8 copy-done.9
  5.7 0.7 copy-done.11
  6.4 0.7 copy-done.13
  7.1 0.7 copy-done.15
  7.7 0.7 copy-done.17
  8.4 0.0 copy-start.12
  8.4 0.0 copy-start.14
  8.4 0.0 copy-start.16
  8.4 0.0 copy-start.18
  8.5 8.4 %shard_map.156 = (bf16[512,1024]{1,0:T(8,128)(2,1)S(1)}, f32[512,1024]{1,0:T(8,128)S(1)}, bf16[2,2,8,256,256]{4,3,2,1,0:T(8,128)(2,1)}) custom-call(f32[16]{0:T(128)S(1)} %copy-done.13, f32[16]{0:T(128)S(1)} %copy-done.15, f32[16]{0:T(128)S(1)} %copy-done.17, bf16[512,1024]{1,0:T(8,128)(2,1)S(1)} %copy-done.3, bf16[512,1024]{1,0:T(8,128)(2,1)S(1)} %copy-done, ...), custom_call_target="tpu_custom_call" | custom-call | tf_op jit(solution)/shard_map/pallas_call | solution.py:532
  16.9 1.0 copy-done.4
  17.8 147.4 %shard_map.157 = (f32[512,1024]{1,0:T(8,128)}, bf16[2,4,4,2,32,1024]{5,4,3,2,1,0:T(8,128)(2,1)}, f32[32,1024]{1,0:T(8,128)}, f32[32,1024]{1,0:T(8,128)}) custom-call(bf16[512,1024]{1,0:T(8,128)(2,1)} %copy-done.4, bf16[2048,1024]{1,0:T(8,128)(2,1)} %bitcast.8, bf16[128,2048]{1,0:T(8,128)(2,1)} %target.1, f32[32,1024]{1,0:T(8,128)} %global_own.1, ...), custom_call_target="tpu_custom_call" | custom-call | tf_op jit(solution)/shard_map/pallas_call | solution.py:356
  165.2 0.0 copy-done.1
  165.2 0.0 copy-done.6
  165.2 0.0 copy-done.8
  165.3 0.0 copy-done.10
  165.3 0.0 copy-done.12
  165.3 0.0 copy-done.14
  165.3 0.0 copy-done.16
  165.3 0.0 copy-done.18
  165.3 0.0 copy-start.2
  165.3 1.6 copy-done.2
  166.9 6.4 %shard_map.158 = bf16[512,1024]{1,0:T(8,128)(2,1)} custom-call(f32[16]{0:T(128)S(1)} %copy-done.14, f32[16]{0:T(128)S(1)} %copy-done.16, f32[16]{0:T(128)S(1)} %copy-done.18, f32[512,1024]{1,0:T(8,128)S(1)} %copy-done.2, f32[512,1024]{1,0:T(8,128)S(1)} %get-tuple-element.13.gated_ref, bf16[512,1024]{1,0:T(8,128)(2,1)S(1)} %copy-done.1, ...), custom_call_target="tpu_custom_call" | custom-call | tf_op jit(solution)/shard_map/pallas_call | solution.py:548
  173.3 0.0 copy-done.19
  173.3 2.0 %copy.20 = bf16[2048,1024]{1,0:T(8,128)(2,1)} copy(bf16[2048,1024]{1,0:T(8,128)(2,1)S(1)} %bitcast.9) | data formatting | bytes 8388608
  175.3 0.7 copy.21
  176.0 0.7 copy.22
  (18 shorter events, 0.0 us)
Async XLA Ops:
  0.6 1.2 copy-start
  1.9 1.2 copy-start.3
  3.1 0.9 copy-start.5
  4.0 0.9 copy-start.7
  5.0 0.8 copy-start.9
  5.7 0.7 copy-start.11
  6.4 0.7 copy-start.13
  7.1 0.7 copy-start.15
  7.7 0.7 copy-start.17
  8.4 156.8 %copy-start.1 = (bf16[512,1024]{1,0:T(8,128)(2,1)S(1)}, bf16[512,1024]{1,0:T(8,128)(2,1)}, u32[]{:S(2)}) copy-start(bf16[512,1024]{1,0:T(8,128)(2,1)} %z_ref.3) | copy-start | bytes 3145732
  8.4 156.8 %copy-start.6 = (bf16[512,256]{1,0:T(8,128)(2,1)S(1)}, bf16[512,256]{1,0:T(8,128)(2,1)}, u32[]{:S(2)}) copy-start(bf16[512,256]{1,0:T(8,128)(2,1)} %b_ref.3) | copy-start | bytes 786436
  8.4 156.8 %copy-start.8 = (bf16[512,256]{1,0:T(8,128)(2,1)S(1)}, bf16[512,256]{1,0:T(8,128)(2,1)}, u32[]{:S(2)}) copy-start(bf16[512,256]{1,0:T(8,128)(2,1)} %c_ref.3) | copy-start | bytes 786436
  8.4 156.9 %copy-start.10 = (f32[512,16]{0,1:T(8,128)S(1)}, f32[512,16]{0,1:T(8,128)}, u32[]{:S(2)}) copy-start(f32[512,16]{0,1:T(8,128)} %param.17) | copy-start | bytes 98308
  8.4 156.9 %copy-start.12 = (f32[1024]{0:T(1024)S(1)}, f32[1024]{0:T(1024)}, u32[]{:S(2)}) copy-start(f32[1024]{0:T(1024)} %param.21) | copy-start | bytes 12292
  8.4 156.9 %copy-start.14 = (f32[16]{0:T(128)S(1)}, f32[16]{0:T(128)}, u32[]{:S(2)}) copy-start(f32[16]{0:T(128)} %a_log.3) | copy-start | bytes 196
  8.4 156.9 %copy-start.16 = (f32[16]{0:T(128)S(1)}, f32[16]{0:T(128)}, u32[]{:S(2)}) copy-start(f32[16]{0:T(128)} %dt_bias.3) | copy-start | bytes 196
  8.4 156.9 %copy-start.18 = (f32[16]{0:T(128)S(1)}, f32[16]{0:T(128)}, u32[]{:S(2)}) copy-start(f32[16]{0:T(128)} %skip.3) | copy-start | bytes 196
  16.9 1.0 copy-start.4
  165.3 1.6 copy-start.2
  166.9 6.4 %copy-start.19 = (bf16[2,4,4,2,32,1024]{5,4,3,2,1,0:T(8,128)(2,1)S(1)}, bf16[2,4,4,2,32,1024]{5,4,3,2,1,0:T(8,128)(2,1)}, u32[]{:S(2)}) copy-start(bf16[2,4,4,2,32,1024]{5,4,3,2,1,0:T(8,128)(2,1)} %get-tuple-element.15) | copy-start | bytes 12582916
  173.3 2.0 %copy-start.21 = (f32[32,1024]{1,0:T(8,128)S(1)}, f32[32,1024]{1,0:T(8,128)}, u32[]{:S(2)}) copy-start(f32[32,1024]{1,0:T(8,128)} %get-tuple-element.24) | copy-start | bytes 393220
  173.3 2.7 %copy-start.20 = (f32[32,1024]{1,0:T(8,128)S(1)}, f32[32,1024]{1,0:T(8,128)}, u32[]{:S(2)}) copy-start(f32[32,1024]{1,0:T(8,128)} %get-tuple-element.25) | copy-start | bytes 393220

commit v3 on v2

--- a/solution.py
+++ b/solution.py
@@ -24,7 +24,7 @@
 WIDTH = 1024
 ENTRIES = 2048 * 4096
 KINDS = ("far", "near", "mid", "ahead", "behind", "relay")
-LAGS = (0, 3, 4, 5, 6, 7, 8)
+LAGS = (0, 2, 3, 4, 5, 6, 7)
 
 
 def exchange_kernel(
@@ -35,6 +35,7 @@
     momentum_own,
     d_normed,
     full,
+    factor_out,
     new_global,
     new_momentum,
     part,
@@ -51,9 +52,10 @@
     r_x,
     s_x,
     r_y,
-    s_y,
     s_z,
     r_z,
+    whole_global,
+    delta,
     sq_a,
     sq_b,
     sq_c,
@@ -67,6 +69,8 @@
     y_recv,
     zl_send,
     zl_recv,
+    early_send,
+    early_recv,
     a_send,
     a_recv,
     b_send,
@@ -229,33 +233,139 @@
             total = total + r_x[u, k - 1].astype(jnp.float32)
         s_x[u] = total.astype(jnp.bfloat16)
 
-    d_normed[...] = jnp.zeros_like(d_normed)
-    stages = list(zip((begin, pass_on, own, relay, gradients, over_x, after_x), LAGS))
-
-    @pl.loop(0, UNITS + LAGS[-1])
-    def _(k):
-        for stage, lag in stages:
-
-            @pl.when((k >= lag) & (k < UNITS + lag))
-            def _():
-                stage(k - lag)
-
-    for half in range(2):
+    def zl_copy(half):
+        return remote(s_z.at[half], r_z.at[half], zl_send.at[half], zl_recv.at[half], on_z(1, 0))
+
+    def early_copies():
+        base = full.at[0, zl, y, x, c]
+        return (
+            remote(base, base, early_send.at[0], early_recv.at[0], on_z(1, 0)),
+            remote(
+                global_own, whole_global.at[zl], early_send.at[1], early_recv.at[1], on_z(1, 0)
+            ),
+        )
+
+    left, right = pl.ds(0, WIDTH // 2), pl.ds(WIDTH // 2, WIDTH // 2)
+
+    def gather(which, half, index, src, device):
+        row = which * 2 + half
+        return remote(src, src, g_send.at[row, index], g_recv.at[row, index], device)
+
+    def near_copies(which, half):
+        piece = full.at[which, half]
+        copies = []
+        for k in range(1, 4):
+            copies.append(gather(which, half, k - 1, piece.at[y, x, c, :, left], on_y(k)))
+            copies.append(gather(which, half, k + 2, piece.at[y, x, c, :, right], on_x(k, 0)))
+        return copies
+
+    def far_copies(which, half, k):
+        piece = full.at[which, half]
+        return (
+            gather(which, half, k + 5, piece.at[:, x, c, :, left], on_x(k, 0)),
+            gather(which, half, k + 8, piece.at[y, :, c, :, right], on_y(k)),
+        )
+
+    def across_copies(which, half, k):
+        piece = full.at[which, half]
+        from_x, from_y = lax.rem(x + 4 - k, 4), lax.rem(y + 4 - k, 4)
+        return (
+            gather(which, half, 12 + k, piece.at[:, from_x, c, :, left], on_x(0, 1)),
+            gather(which, half, 16 + k, piece.at[from_y, :, c, :, right], on_x(0, 1)),
+        )
+
+    def near_start(which, half):
+        for copy in near_copies(which, half):
+            copy.start()
+
+    def far_start(which, half):
+        for copy in near_copies(which, half):
+            copy.wait_recv()
+        for k in (1, 3, 2):
+            for copy in far_copies(which, half, k):
+                copy.start()
+        for copy in across_copies(which, half, 0):
+            copy.start()
+
+    def across_start(which, half):
+        for k in (1, 3, 2):
+            for arrived, copy in zip(far_copies(which, half, k), across_copies(which, half, k)):
+                arrived.wait_recv()
+                copy.start()
+
+    def y_start(half):
         for k in range(1, 4):
             y_copy(half, k).start()
-    for half in range(2):
+
+    def after_y(half):
         total = s_x[half * 4 + y].astype(jnp.float32)
         for k in range(1, 4):
             y_copy(half, k).wait_recv()
             total = total + r_y[half, k - 1].astype(jnp.float32)
-        s_y[half] = total
-    s_z[...] = s_y[1 - zl].astype(jnp.bfloat16)
-    over_z = remote(s_z, r_z, zl_send.at[0], zl_recv.at[0], on_z(1, 0))
-    over_z.start()
-    over_z.wait_recv()
-    delta = global_own[...] - (s_y[zl] + r_z[...].astype(jnp.float32)) * (1.0 / 64)
-
-    squares = jnp.sum((delta * delta).reshape(4, 8, WIDTH), axis=0)
+        s_z[half] = total.astype(jnp.bfloat16)
+        zl_copy(half).start()
+
+    def settle(half):
+        zl_copy(half).wait_recv()
+        total = s_z[half].astype(jnp.float32) + r_z[half].astype(jnp.float32)
+        change = whole_global[half] - total * (1.0 / 64)
+        delta[half] = change
+        full[1, half, y, x, c] = change.astype(jnp.bfloat16)
+        near_start(1, half)
+
+    def early_near():
+        for copy in early_copies():
+            copy.wait_recv()
+        near_start(0, 0)
+        near_start(0, 1)
+
+    def early_far():
+        far_start(0, 0)
+        far_start(0, 1)
+
+    def early_across():
+        across_start(0, 0)
+        across_start(0, 1)
+
+    whole_global[zl] = global_own[...]
+    base = global_own[...] - (outer_rate * outer_beta * outer_beta) * momentum_own[...]
+    full[0, zl, y, x, c] = base.astype(jnp.bfloat16)
+    d_normed[...] = jnp.zeros_like(d_normed)
+    for copy in early_copies():
+        copy.start()
+    stages = list(zip((begin, pass_on, own, relay, gradients, over_x, after_x), LAGS))
+    middle = LAGS[-1] + UNITS // 2
+    events = (
+        (3, early_near),
+        (4, early_far),
+        (5, early_across),
+        (middle, lambda: y_start(0)),
+        (middle + 1, lambda: after_y(0)),
+        (middle + 2, lambda: settle(0)),
+        (middle + 3, lambda: far_start(1, 0)),
+    )
+
+    @pl.loop(0, UNITS + LAGS[-1])
+    def _(k):
+        for stage, lag in stages:
+
+            @pl.when((k >= lag) & (k < UNITS + lag))
+            def _():
+                stage(k - lag)
+
+        for when, event in events:
+
+            @pl.when(k == when)
+            def _():
+                event()
+
+    y_start(1)
+    across_start(1, 0)
+    after_y(1)
+    settle(1)
+
+    change = delta[zl]
+    squares = jnp.sum((change * change).reshape(4, 8, WIDTH), axis=0)
     folded = squares[:, :128]
     for first in range(128, WIDTH, 128):
         folded = folded + squares[:, first : first + 128]
@@ -275,6 +385,7 @@
     ]
     for copy in b_copies:
         copy.start()
+    far_start(1, 1)
     for copy in b_copies:
         copy.wait_recv()
     sq_c[zl, j] = jnp.sum(sq_b[...], axis=0)
@@ -284,60 +395,32 @@
     ]
     for copy in c_copies:
         copy.start()
+    across_start(1, 1)
     for copy in c_copies:
         copy.wait_recv()
     square_sum = jnp.sum(jnp.sum(sq_c[...].reshape(8, 8, 128), axis=0), keepdims=True)
     factor = jnp.minimum(1.0, clip_rms / jnp.sqrt(square_sum / ENTRIES + 1e-06))
-    clipped = factor * delta
+    factor_out[...] = jnp.broadcast_to(factor, factor_out.shape)
+    clipped = factor * change
     moment = outer_beta * momentum_own[...] + clipped
-    moved = global_own[...] - outer_rate * (clipped + outer_beta * moment)
     new_momentum[...] = moment
-    new_global[...] = moved
-    full[zl, y, x, c] = moved.astype(jnp.bfloat16)
-
-    def gather(index, src, device):
-        return remote(src, src, g_send.at[index], g_recv.at[index], device)
-
-    mine = full.at[zl, y, x, c]
-    first = gather(0, mine, on_z(1, 0))
-    first.start()
-    first.wait_recv()
-    left, right = pl.ds(0, WIDTH // 2), pl.ds(WIDTH // 2, WIDTH // 2)
-    near = [gather(k, full.at[:, y, x, c, :, left], on_y(k)) for k in range(1, 4)]
-    near += [gather(3 + k, full.at[:, y, x, c, :, right], on_x(k, 0)) for k in range(1, 4)]
-    for copy in near:
-        copy.start()
-    for copy in near:
-        copy.wait_recv()
-    far = [gather(6 + k, full.at[:, :, x, c, :, left], on_x(k, 0)) for k in range(1, 4)]
-    far += [gather(9 + k, full.at[:, y, :, c, :, right], on_y(k)) for k in range(1, 4)]
-    for i in (0, 3, 2, 5, 1, 4):
-        far[i].start()
-
-    def to_core(index, k):
-        if index < 4:
-            src = full.at[:, :, lax.rem(x + 4 - k, 4), c, :, left]
-        else:
-            src = full.at[:, lax.rem(y + 4 - k, 4), :, c, :, right]
-        return gather(13 + index, src, on_x(0, 1))
-
-    across = [to_core(0, 0), to_core(4, 0)]
-    for copy in across:
-        copy.start()
-    for k in (1, 3, 2):
-        for base in (0, 3):
-            far[base + k - 1].wait_recv()
-            copy = to_core(k if base == 0 else 4 + k, k)
-            copy.start()
-            across.append(copy)
-    for copy in across:
-        copy.wait_recv()
-
-    for copy in [over_z, first, *a_copies, *b_copies, *c_copies, *near, *far, *across]:
+    new_global[...] = global_own[...] - outer_rate * (clipped + outer_beta * moment)
+
+    for copy in [*a_copies, *b_copies, *c_copies, *early_copies()]:
         copy.wait_send()
     for half in range(2):
+        zl_copy(half).wait_send()
         for k in range(1, 4):
             y_copy(half, k).wait_send()
+        for which in range(2):
+            for copy in near_copies(which, half):
+                copy.wait_send()
+            for k in range(4):
+                for copy in across_copies(which, half, k):
+                    copy.wait()
+                if k:
+                    for copy in far_copies(which, half, k):
+                        copy.wait_send()
 
     @pl.loop(0, UNITS)
     def _(u):
@@ -353,16 +436,17 @@
     piece = (UNITS, TOKENS, FEATURES)
     dma = pltpu.SemaphoreType.DMA
     vmem = pl.BlockSpec(memory_space=pltpu.VMEM)
-    d_normed, full, new_global, new_momentum = pl.pallas_call(
+    d_normed, full, factor, new_global, new_momentum = pl.pallas_call(
         exchange_kernel,
         out_shape=(
             jax.ShapeDtypeStruct((4 * TOKENS, WIDTH), jnp.float32),
-            jax.ShapeDtypeStruct((2, 4, 4, 2, 32, WIDTH), half),
+            jax.ShapeDtypeStruct((2, 2, 4, 4, 2, 32, WIDTH), half),
+            jax.ShapeDtypeStruct((8, 128), jnp.float32),
             jax.ShapeDtypeStruct((32, WIDTH), jnp.float32),
             jax.ShapeDtypeStruct((32, WIDTH), jnp.float32),
         ),
         in_specs=[vmem] * 5,
-        out_specs=[vmem] * 4,
+        out_specs=[vmem] * 5,
         scratch_shapes=[
             pltpu.VMEM((UNITS, 4, TOKENS, FEATURES), jnp.float32),
             *[pltpu.VMEM(piece, half)] * 6,
@@ -373,9 +457,10 @@
             pltpu.VMEM((UNITS, 3, 32, WIDTH), half),
             pltpu.VMEM((UNITS, 32, WIDTH), half),
             pltpu.VMEM((2, 3, 32, WIDTH), half),
+            pltpu.VMEM((2, 32, WIDTH), half),
+            pltpu.VMEM((2, 32, WIDTH), half),
             pltpu.VMEM((2, 32, WIDTH), jnp.float32),
-            pltpu.VMEM((32, WIDTH), half),
-            pltpu.VMEM((32, WIDTH), half),
+            pltpu.VMEM((2, 32, WIDTH), jnp.float32),
             pltpu.VMEM((4, 2, 8, 128), jnp.float32),
             pltpu.VMEM((4, 8, 128), jnp.float32),
             pltpu.VMEM((2, 4, 8, 128), jnp.float32),
@@ -383,17 +468,18 @@
             *[dma((UNITS,))] * 2,
             *[dma((UNITS, 3))] * 2,
             *[dma((2, 3))] * 2,
-            *[dma((1,))] * 2,
+            *[dma((2,))] * 2,
+            *[dma((2,))] * 2,
             *[dma((7,))] * 2,
             *[dma((3,))] * 2,
             *[dma((7,))] * 2,
-            *[dma((21,))] * 2,
+            *[dma((4, 20))] * 2,
         ],
         compiler_params=pltpu.CompilerParams(
-            collective_id=0, has_side_effects=True, vmem_limit_bytes=60 * 2**20
+            collective_id=0, has_side_effects=True, vmem_limit_bytes=67043328
         ),
     )(normed, weight, target, global_own, momentum_own)
-    return d_normed, full.reshape(2048, WIDTH), new_global, new_momentum
+    return d_normed, full.reshape(2, 2048, WIDTH), factor, new_global, new_momentum
 
 
 def head_scalars(ref, first, tokens):
@@ -477,8 +563,37 @@
 
 
 def backward_kernel(
-    a_log, dt_bias, skip, dn_ref, gated_ref, z_ref, w_ref, b_ref, c_ref, dt_ref, gain_ref, out_ref
+    a_log,
+    dt_bias,
+    skip,
+    dn_ref,
+    gated_ref,
+    z_ref,
+    w_ref,
+    b_ref,
+    c_ref,
+    dt_ref,
+    gain_ref,
+    pair_ref,
+    factor_ref,
+    global_ref,
+    momentum_ref,
+    out_ref,
+    weight_ref,
+    new_global,
+    new_momentum,
 ):
+    new_global[...] = global_ref[...]
+    new_momentum[...] = momentum_ref[...]
+    share = factor_ref[0:1, 0:1] * (outer_rate * (1.0 + outer_beta))
+
+    @pl.loop(0, 16)
+    def _(i):
+        part = pl.ds(pl.multiple_of(i * 64, 64), 64)
+        base = pair_ref[0, part].astype(jnp.float32)
+        change = pair_ref[1, part].astype(jnp.float32)
+        weight_ref[part] = (base - share * change).astype(jnp.bfloat16)
+
     first = pl.program_id(0) * 8
     _, steps, by_row, by_column = decays(dt_ref, a_log, dt_bias, first)
     low = lax.broadcasted_iota(jnp.int32, (1, 128), 1) < HEAD_DIM
@@ -539,20 +654,37 @@
         ),
         in_specs=[small, small, small, wide, wide, state, state, heads, gain],
         out_specs=[wide, wide, tables],
-        compiler_params=pltpu.CompilerParams(vmem_limit_bytes=48 * 2**20),
+        compiler_params=pltpu.CompilerParams(vmem_limit_bytes=67043328),
     )(a_log, dt_bias, skip_d, x_in, gate_z, b_proj, c_proj, dt, gain_row)
 
 
-def pull_back(d_normed, gated, gate_z, tables_in, b_proj, c_proj, dt, a_log, dt_bias, skip_d, row):
+def pull_back(
+    d_normed, gated, gate_z, tables_in, b_proj, c_proj, dt, a_log, dt_bias, skip_d, row, *outer
+):
     small, wide, state, heads, gain, tables = group_specs()
+    rows = pl.BlockSpec((32, 512), lambda g: (0, g))
     return pl.pallas_call(
         backward_kernel,
         grid=(2,),
-        out_shape=jax.ShapeDtypeStruct((512, WIDTH), jnp.bfloat16),
-        in_specs=[small, small, small, wide, wide, wide, tables, state, state, heads, gain],
-        out_specs=wide,
-        compiler_params=pltpu.CompilerParams(vmem_limit_bytes=48 * 2**20),
-    )(a_log, dt_bias, skip_d, d_normed, gated, gate_z, tables_in, b_proj, c_proj, dt, row)
+        out_shape=(
+            jax.ShapeDtypeStruct((512, WIDTH), jnp.bfloat16),
+            jax.ShapeDtypeStruct((2048, WIDTH), jnp.bfloat16),
+            jax.ShapeDtypeStruct((32, WIDTH), jnp.float32),
+            jax.ShapeDtypeStruct((32, WIDTH), jnp.float32),
+        ),
+        in_specs=[
+            *[small, small, small, wide, wide, wide, tables, state, state, heads, gain],
+            pl.BlockSpec((2, 1024, WIDTH), lambda g: (0, g, 0)),
+            pl.BlockSpec((8, 128), lambda g: (0, 0)),
+            rows,
+            rows,
+        ],
+        out_specs=[wide, pl.BlockSpec((1024, WIDTH), lambda g: (g, 0)), rows, rows],
+        compiler_params=pltpu.CompilerParams(vmem_limit_bytes=67043328),
+    )(
+        *[a_log, dt_bias, skip_d, d_normed, gated, gate_z, tables_in, b_proj, c_proj, dt, row],
+        *outer,
+    )
 
 
 def shards(
@@ -577,11 +709,11 @@
     normed, gated, tables = forward(
         x_in, gate_z, b_proj, c_proj, dt, a_log, dt_bias, skip_d, gain_row
     )
-    d_normed, new_weight, new_global, new_momentum = exchange(
-        normed, local_weight, target, global_weight, momentum
-    )
-    grad_x = pull_back(
-        d_normed, gated, gate_z, tables, b_proj, c_proj, dt, a_log, dt_bias, skip_d, gain_row
+    d_normed, *outer = exchange(normed, local_weight, target, global_weight, momentum)
+    grad_x, new_weight, new_global, new_momentum = pull_back(
+        *[d_normed, gated, gate_z, tables, b_proj, c_proj, dt, a_log, dt_bias, skip_d],
+        gain_row,
+        *outer,
     )
     return (grad_x, new_weight, new_global, new_momentum)
 

time: 177 us -> 163 us (0.921)
  local copies, waits for them, and re-layouts: 13.7 us -> 0 us
    unnamed x47 -> x0, local copies, waits for them, and re-layouts: 13.7 us -> none
    pallas_call x1, Pallas kernels: 147 us -> 142 us  [exchange(): pl.pallas_call(exchange_kernel, out_shape=(jax.ShapeDtypeStruct((4 * TOKE...]
    pallas_call x1, Pallas kernels: 6.42 us -> 11.4 us  [pull_back(): pl.pallas_call(backward_kernel, grid=(2,), out_shape=(jax.ShapeDtypeStruc...]
where the time goes in v3:
time: 163 us
  Pallas kernels  163 us (100%)
    pallas_call x1, Pallas kernels, exchange(): pl.pallas_call(exchange_kernel, out_shape=(jax.ShapeDtypeStruct((4 * TOKE...  142 us
    pallas_call x1, Pallas kernels, pull_back(): pl.pallas_call(backward_kernel, grid=(2,), out_shape=(jax.ShapeDtypeStruc...  11.4 us
    pallas_call x1, Pallas kernels, forward(): pl.pallas_call(forward_kernel, grid=(2,), out_shape=(jax.ShapeDtypeStruct...  9.22 us

profile of v3, /device:TPU:1, one launch (start us, length us, event | category | flops | bytes accessed | tf_op | source)
XLA Modules:
  0.0 163.3 jit_solution(2233681848110138297)
XLA Ops:
  0.6 9.2 %shard_map.156 = (bf16[512,1024]{1,0:T(8,128)(2,1)}, f32[512,1024]{1,0:T(8,128)}, bf16[2,2,8,256,256]{4,3,2,1,0:T(8,128)(2,1)}) custom-call(f32[16]{0:T(128)} %a_log.3, f32[16]{0:T(128)} %dt_bias.3, f32[16]{0:T(128)} %skip.3, bf16[512,1024]{1,0:T(8,128)(2,1)} %x_ref.1, bf16[512,1024]{1,0:T(8,128)(2,1)} %z_ref.3, bf16[512,256]{1,0:T(8,128)(2,1)} %b_ref.3, ...), custom_call_target="tpu_custom_call" | custom-call | tf_op jit(solution)/shard_map/pallas_call | solution.py:647
  9.9 142.1 %shard_map.157 = (f32[512,1024]{1,0:T(8,128)}, bf16[2,2,4,4,2,32,1024]{6,5,4,3,2,1,0:T(8,128)(2,1)}, f32[8,128]{1,0:T(8,128)}, f32[32,1024]{1,0:T(8,128)}, f32[32,1024]{1,0:T(8,128)}) custom-call(bf16[512,1024]{1,0:T(8,128)(2,1)} %get-tuple-element.12.normed, bf16[2048,1024]{1,0:T(8,128)(2,1)} %bitcast.5, bf16[128,2048]{1,0:T(8,128)(2,1)} %target.1, ...), custom_call_target="tpu_custom_call" | custom-call | tf_op jit(solution)/shard_map/pallas_call | solution.py:439
  152.0 11.4 %shard_map.158 = (bf16[512,1024]{1,0:T(8,128)(2,1)}, bf16[2048,1024]{1,0:T(8,128)(2,1)}, f32[32,1024]{1,0:T(8,128)}, f32[32,1024]{1,0:T(8,128)}) custom-call(f32[16]{0:T(128)} %a_log.3, f32[16]{0:T(128)} %dt_bias.3, f32[16]{0:T(128)} %skip.3, f32[512,1024]{1,0:T(8,128)} %get-tuple-element.13.dn_ref, f32[512,1024]{1,0:T(8,128)} %get-tuple-element.14.gated_ref, ...), custom_call_target="tpu_custom_call" | custom-call | tf_op jit(solution)/shard_map/pallas_call | solution.py:666

commit v4 on v1

v4 whole, which is shorter than its diff:
```python
import jax
import jax.numpy as jnp
from jax import lax
from jax.experimental import pallas as pl
from jax.experimental.pallas import tpu as pltpu
from jax.sharding import Mesh
from jax.sharding import PartitionSpec as P

HEAD_DIM = 64
STATE = 128
SPAN = 256
REPLICA = ("replica_0", "replica_1", "replica_2", "replica_3")
REPLICA_TENSOR = ("replica_0", "replica_1", "replica_2", "replica_3", "tensor")


inner_rate = 0.001
outer_rate = 0.7
outer_beta = 0.9
clip_rms = 0.005
MESH = pl.DeviceIdType.MESH
UNITS = 8
FEATURES = 256
TOKENS = 128
WIDTH = 1024
ENTRIES = 2048 * 4096
KINDS = ("far", "near", "mid", "ahead", "behind", "relay")
ORDER = (
    ("begin", 0),
    ("begin", 1),
    ("begin", 2),
    ("begin", 3),
    ("begin", 4),
    ("pass", 0),
    ("begin", 5),
    ("begin", 6),
    ("pass", 2),
    ("early_near",),
    ("begin", 7),
    ("pass", 1),
    ("pass", 4),
    ("early_far",),
    ("own", 0),
    ("pass", 3),
    ("pass", 6),
    ("own", 2),
    ("pass", 5),
    ("early_across",),
    ("own", 4),
    ("pass", 7),
    ("own", 1),
    ("own", 6),
    ("relay", 0),
    ("own", 3),
    ("relay", 2),
    ("own", 5),
    ("relay", 1),
    ("relay", 4),
    ("own", 7),
    ("relay", 3),
    ("relay", 5),
    ("grad", 1),
    ("relay", 6),
    ("grad", 0),
    ("relay", 7),
    ("ox", 1),
    ("grad", 3),
    ("ox", 0),
    ("grad", 2),
    ("ox", 3),
    ("ax", 1),
    ("grad", 5),
    ("ox", 2),
    ("ax", 0),
    ("grad", 4),
    ("ox", 5),
    ("ax", 3),
    ("grad", 7),
    ("ox", 4),
    ("ax", 2),
    ("ys", 0),
    ("grad", 6),
    ("ox", 7),
    ("bwd", 1),
    ("ox", 6),
    ("ay", 0),
    ("ax", 4),
    ("ax", 5),
    ("bwd", 0),
    ("se", 0),
    ("ax", 7),
    ("ax", 6),
    ("ys", 1),
    ("far", 0),
    ("ay", 1),
    ("se", 1),
    ("a",),
    ("ac", 0),
    ("b",),
    ("far", 1),
    ("c",),
    ("fin",),
    ("ac", 1),
)


def head_scalars(ref, first, tokens):
    row = lax.broadcasted_iota(jnp.int32, (8, tokens), 0)
    out = jnp.zeros((8, tokens), jnp.float32)
    for r in range(8):
        out = jnp.where(row == r, ref[first + r], out)
    return out


def dot(a, b, over, **settings):
    return lax.dot_general(
        a, b, ((over[:1], over[1:]), ((), ())), preferred_element_type=jnp.float32, **settings
    )


def decays(dt, a_log, dt_bias, first):
    tokens = dt.shape[1]
    raw = dt[...] + head_scalars(dt_bias, first, tokens)
    step = jnp.maximum(raw, 0.0) + jnp.log1p(jnp.exp(-jnp.abs(raw)))
    rate = -jnp.exp(head_scalars(a_log, first, tokens)) * step
    below = lax.broadcasted_iota(jnp.int32, (SPAN, SPAN), 0) >= lax.broadcasted_iota(
        jnp.int32, (SPAN, SPAN), 1
    )
    ones = jnp.where(below, 1.0, 0.0)
    steps, by_row, by_column = [], [], []
    for k in range(2):
        own = rate[:, k * SPAN : (k + 1) * SPAN]
        steps.append(step[:, k * SPAN : (k + 1) * SPAN])
        by_row.append(dot(own, ones, (1, 1), precision=lax.Precision.HIGHEST))
        by_column.append(dot(ones, own, (1, 1), precision=lax.Precision.HIGHEST))
    return below, steps, by_row, by_column


def tail_keys(keys, step, cum):
    weight = jnp.exp(cum[:, SPAN - 1 :] - cum) * step
    turned = keys.astype(jnp.float32).T
    return [(turned * weight[r : r + 1]).astype(jnp.bfloat16) for r in range(8)]


def paired(low, one, two):
    return jnp.where(low, one, two)


def forward_group(
    g, a_log, dt_bias, skip, x_all, z_all, b_all, c_all, dt_all, gain_all, normed, gated_all, tables
):
    first = g * 8
    wide = pl.ds(pl.multiple_of(g * 512, 512), 512)
    narrow = pl.ds(pl.multiple_of(g * STATE, STATE), STATE)
    x_ref, z_ref = x_all.at[:, wide], z_all.at[:, wide]
    b_ref, c_ref = b_all.at[:, narrow], c_all.at[:, narrow]
    dt_ref = dt_all.at[pl.ds(pl.multiple_of(first, 8), 8)]
    gain_ref, normed_ref, gated_ref = gain_all.at[:, wide], normed.at[:, wide], gated_all.at[:, wide]
    below, steps, by_row, by_column = decays(dt_ref, a_log, dt_bias, first)
    low = lax.broadcasted_iota(jnp.int32, (1, 128), 1) < HEAD_DIM
    tails = tail_keys(b_ref[:SPAN], steps[0], by_row[0])
    for k in range(2):
        rows = slice(k * SPAN, (k + 1) * SPAN)
        scores = dot(c_ref[rows], b_ref[rows], (1, 1))
        squares = jnp.zeros((SPAN, 1), jnp.float32)
        for q in range(4):
            cols = slice(q * 128, (q + 1) * 128)
            values = x_ref[rows, cols]
            sides = []
            for r in (2 * q, 2 * q + 1):
                gap = by_column[k][:, r : r + 1] - by_row[k][r : r + 1]
                table = jnp.where(below, jnp.exp(gap), 0.0)
                weights = (scores * table * steps[k][r : r + 1]).astype(jnp.bfloat16)
                tables[g, k, r] = weights
                sides.append(dot(weights, values, (1, 0)))
            skips = paired(low, skip[first + 2 * q], skip[first + 2 * q + 1])
            out = paired(low, *sides) + skips * values.astype(jnp.float32)
            if k == 1:
                earlier = x_ref[:SPAN, cols]
                state = paired(low, *[dot(tails[r], earlier, (1, 0)) for r in (2 * q, 2 * q + 1)])
                fade = jnp.exp(
                    paired(low, *[by_column[1][:, r : r + 1] for r in (2 * q, 2 * q + 1)])
                )
                out = out + dot(c_ref[rows], state.astype(jnp.bfloat16), (1, 0)) * fade
            z = z_ref[rows, cols].astype(jnp.float32)
            gated = out * (z / (1.0 + jnp.exp(-z)))
            gated_ref[rows, cols] = gated
            squares = squares + jnp.sum(gated * gated, axis=1, keepdims=True)
        scale = lax.rsqrt(squares * (1.0 / 512) + 1e-05)
        normed_ref[rows] = (gated_ref[rows] * scale * gain_ref[...]).astype(jnp.bfloat16)


def backward_group(
    g, a_log, dt_bias, skip, dn_all, gated_all, z_all, tables, b_all, c_all, dt_all, gain_all, grad
):
    first = g * 8
    wide, narrow = slice(g * 512, g * 512 + 512), slice(g * STATE, g * STATE + STATE)
    dn_ref, gated_ref, z_ref = dn_all.at[:, wide], gated_all.at[:, wide], z_all.at[:, wide]
    b_ref, c_ref, dt_ref = b_all.at[:, narrow], c_all.at[:, narrow], dt_all.at[first : first + 8]
    gain_ref, out_ref = gain_all.at[:, wide], grad.at[:, wide]
    _, steps, by_row, by_column = decays(dt_ref, a_log, dt_bias, first)
    low = lax.broadcasted_iota(jnp.int32, (1, 128), 1) < HEAD_DIM
    tails = tail_keys(b_ref[:SPAN], steps[0], by_row[0])
    states = []
    for k in (1, 0):
        rows = slice(k * SPAN, (k + 1) * SPAN)
        gated = gated_ref[rows]
        pulled = dn_ref[rows] * gain_ref[...]
        mean = jnp.sum(gated * gated, axis=1, keepdims=True) * (1.0 / 512)
        scale = lax.rsqrt(mean + 1e-05)
        along = jnp.sum(gated * pulled, axis=1, keepdims=True) * (1.0 / 512)
        fall = along * scale * scale
        for q in range(4):
            cols = slice(q * 128, (q + 1) * 128)
            z = z_ref[rows, cols].astype(jnp.float32)
            own = dn_ref[rows, cols] * gain_ref[:, cols] - gated_ref[rows, cols] * fall
            ssd = own * scale * (z / (1.0 + jnp.exp(-z)))
            short = ssd.astype(jnp.bfloat16)
            sides = [dot(tables[g, k, r], short, (0, 0)) for r in (2 * q, 2 * q + 1)]
            skips = paired(low, skip[first + 2 * q], skip[first + 2 * q + 1])
            grad = paired(low, *sides) + skips * ssd
            if k == 1:
                fade = jnp.exp(
                    paired(low, *[by_column[1][:, r : r + 1] for r in (2 * q, 2 * q + 1)])
                )
                states.append(
                    dot(c_ref[rows], (ssd * fade).astype(jnp.bfloat16), (0, 0)).astype(
                        jnp.bfloat16
                    )
                )
            else:
                grad = grad + paired(
                    low, *[dot(tails[r], states[q], (0, 0)) for r in (2 * q, 2 * q + 1)]
                )
            out_ref[rows, cols] = grad.astype(jnp.bfloat16)


def step_kernel(
    a_log,
    dt_bias,
    skip,
    x_ref,
    z_ref,
    b_ref,
    c_ref,
    dt_ref,
    gain_ref,
    weight_in,
    target,
    global_own,
    momentum_own,
    grad_x,
    new_weight,
    new_global,
    new_momentum,
    weight,
    normed,
    gated,
    tables,
    d_normed,
    full,
    part,
    s_far,
    s_near,
    s_mid,
    r_far,
    r_near,
    r_mid,
    cot,
    fresh,
    r_core,
    s_core,
    r_x,
    s_x,
    r_y,
    s_z,
    r_z,
    whole_global,
    delta,
    sq_a,
    sq_b,
    sq_c,
    share,
    weight_sem,
    z_send,
    z_recv,
    core_send,
    core_recv,
    x_send,
    x_recv,
    y_send,
    y_recv,
    zl_send,
    zl_recv,
    early_send,
    early_recv,
    a_send,
    a_recv,
    b_send,
    b_recv,
    c_send,
    c_recv,
    g_send,
    g_recv,
):
    zl = lax.axis_index("replica_0")
    y = lax.axis_index("replica_1")
    x = lax.axis_index("replica_2")
    c = lax.axis_index("replica_3")
    j = lax.axis_index("tensor")

    def on_z(kz, kj):
        return {"replica_0": lax.rem(zl + kz, 2), "tensor": lax.rem(j + kj, 4)}

    def on_x(kx, kc):
        return {"replica_2": lax.rem(x + kx, 4), "replica_3": lax.rem(c + kc, 2)}

    def on_y(ky):
        return {"replica_1": lax.rem(y + ky, 4)}

    z_peers = [(kz, kj) for kz in range(2) for kj in range(4) if kz + kj]
    x_peers = [(kx, kc) for kx in range(4) for kc in range(2) if kx + kc]
    barrier = pltpu.get_barrier_semaphore()
    for kz, kj in z_peers:
        pl.semaphore_signal(barrier, inc=1, device_id=on_z(kz, kj), device_id_type=MESH)
    for kx, kc in x_peers:
        pl.semaphore_signal(barrier, inc=1, device_id=on_x(kx, kc), device_id_type=MESH)
    for ky in range(1, 4):
        pl.semaphore_signal(barrier, inc=1, device_id=on_y(ky), device_id_type=MESH)
    fetch = pltpu.make_async_copy(weight_in, weight, weight_sem)
    fetch.start()

    @pl.loop(0, 2)
    def _(g):
        forward_group(
            *[g, a_log, dt_bias, skip, x_ref, z_ref, b_ref, c_ref, dt_ref, gain_ref],
            *[normed, gated, tables],
        )

    pl.semaphore_wait(barrier, len(z_peers) + len(x_peers) + 3)
    fetch.wait()

    def remote(src, dst, send_sem, recv_sem, device):
        return pltpu.make_async_remote_copy(
            src_ref=src,
            dst_ref=dst,
            send_sem=send_sem,
            recv_sem=recv_sem,
            device_id=device,
            device_id_type=MESH,
        )

    def way(u):
        return 1 - 2 * (u % 2)

    def shard(step):
        return lax.rem(j + step + 4, 4)

    def z_copy(kind, u):
        d = way(u)
        ahead = {"tensor": shard(d)}
        behind = {"tensor": shard(-d)}
        src, dst, device = {
            "far": lambda: (s_far.at[u], r_far.at[u], behind),
            "near": lambda: (s_near.at[u], r_near.at[u], ahead),
            "mid": lambda: (s_mid.at[u], r_mid.at[u], behind),
            "ahead": lambda: (cot.at[u, j], cot.at[u, j], ahead),
            "behind": lambda: (cot.at[u, j], cot.at[u, j], behind),
            "relay": lambda: (cot.at[u, shard(-d)], cot.at[u, shard(-d)], ahead),
        }[kind]()
        slot = KINDS.index(kind)
        return remote(src, dst, z_send.at[u, slot], z_recv.at[u, slot], device)

    def core_copy(u):
        return remote(
            fresh.at[u, :, 1 - c],
            r_core.at[u],
            core_send.at[u],
            core_recv.at[u],
            {"replica_3": 1 - c},
        )

    def x_copy(u, k):
        there = lax.rem(x + k, 4)
        return remote(
            s_core.at[u, there],
            r_x.at[u, k - 1],
            x_send.at[u, k - 1],
            x_recv.at[u, k - 1],
            {"replica_2": there},
        )

    def y_copy(half, k):
        there = lax.rem(y + k, 4)
        return remote(
            s_x.at[half * 4 + there],
            r_y.at[half, k - 1],
            y_send.at[half, k - 1],
            y_recv.at[half, k - 1],
            {"replica_1": there},
        )

    def rows_of(u):
        return slice(u * FEATURES, (u + 1) * FEATURES)

    def begin(u):
        d = way(u)
        products = lax.dot_general(
            normed[...],
            weight[rows_of(u), :],
            (((1,), (1,)), ((), ())),
            preferred_element_type=jnp.float32,
        )
        part[u] = products.reshape(4, TOKENS, FEATURES)
        s_far[u] = part[u, shard(2)].astype(jnp.bfloat16)
        s_near[u] = part[u, shard(d)].astype(jnp.bfloat16)
        z_copy("far", u).start()
        z_copy("near", u).start()

    def pass_on(u):
        z_copy("far", u).wait_recv()
        s_mid[u] = (r_far[u].astype(jnp.float32) + part[u, shard(-way(u))]).astype(jnp.bfloat16)
        z_copy("mid", u).start()

    def own(u):
        z_copy("near", u).wait_recv()
        z_copy("mid", u).wait_recv()
        total = part[u, j] + r_near[u].astype(jnp.float32) + r_mid[u].astype(jnp.float32)
        cot[u, j] = (total - target[:, rows_of(u)].astype(jnp.float32)).astype(jnp.bfloat16)
        z_copy("ahead", u).start()
        z_copy("behind", u).start()

    def relay(u):
        z_copy("ahead", u).wait_recv()
        z_copy("relay", u).start()

    def gradients(u):
        z_copy("behind", u).wait_recv()
        z_copy("relay", u).wait_recv()
        whole = cot[u].reshape(4 * TOKENS, FEATURES)
        for first in range(0, WIDTH, 512):
            cols = slice(first, first + 512)
            rows = weight[rows_of(u), cols]
            grad = lax.dot_general(
                whole,
                normed[:, cols],
                (((0,), (0,)), ((), ())),
                preferred_element_type=jnp.float32,
            )
            moved = (rows.astype(jnp.float32) - inner_rate * grad).astype(jnp.bfloat16)
            fresh[u, :, :, :, cols] = moved.reshape(4, 2, 32, 512)
            d_normed[:, cols] += jnp.dot(whole, rows, preferred_element_type=jnp.float32)
        core_copy(u).start()

    def over_x(u):
        core_copy(u).wait_recv()
        for i in range(4):
            both = fresh[u, i, c].astype(jnp.float32) + r_core[u, i].astype(jnp.float32)
            s_core[u, i] = both.astype(jnp.bfloat16)
        for k in range(1, 4):
            x_copy(u, k).start()

    def after_x(u):
        total = s_core[u, x].astype(jnp.float32)
        for k in range(1, 4):
            x_copy(u, k).wait_recv()
            total = total + r_x[u, k - 1].astype(jnp.float32)
        s_x[u] = total.astype(jnp.bfloat16)

    def zl_copy(half):
        return remote(s_z.at[half], r_z.at[half], zl_send.at[half], zl_recv.at[half], on_z(1, 0))

    def early_copies():
        base = full.at[0, zl, y, x, c]
        return (
            remote(base, base, early_send.at[0], early_recv.at[0], on_z(1, 0)),
            remote(
                global_own, whole_global.at[zl], early_send.at[1], early_recv.at[1], on_z(1, 0)
            ),
        )

    left, right = pl.ds(0, WIDTH // 2), pl.ds(WIDTH // 2, WIDTH // 2)

    def gather(which, half, index, src, device):
        row = which * 2 + half
        return remote(src, src, g_send.at[row, index], g_recv.at[row, index], device)

    def near_copies(which, half):
        piece = full.at[which, half]
        copies = []
        for k in range(1, 4):
            copies.append(gather(which, half, k - 1, piece.at[y, x, c, :, left], on_y(k)))
            copies.append(gather(which, half, k + 2, piece.at[y, x, c, :, right], on_x(k, 0)))
        return copies

    def far_copies(which, half, k):
        piece = full.at[which, half]
        return (
            gather(which, half, k + 5, piece.at[:, x, c, :, left], on_x(k, 0)),
            gather(which, half, k + 8, piece.at[y, :, c, :, right], on_y(k)),
        )

    def across_copies(which, half, k):
        piece = full.at[which, half]
        from_x, from_y = lax.rem(x + 4 - k, 4), lax.rem(y + 4 - k, 4)
        return (
            gather(which, half, 12 + k, piece.at[:, from_x, c, :, left], on_x(0, 1)),
            gather(which, half, 16 + k, piece.at[from_y, :, c, :, right], on_x(0, 1)),
        )

    def near_start(which, half):
        for copy in near_copies(which, half):
            copy.start()

    def far_start(which, half):
        for copy in near_copies(which, half):
            copy.wait_recv()
        for k in (1, 3, 2):
            for copy in far_copies(which, half, k):
                copy.start()
        for copy in across_copies(which, half, 0):
            copy.start()

    def across_start(which, half):
        for k in (1, 3, 2):
            for arrived, copy in zip(far_copies(which, half, k), across_copies(which, half, k)):
                arrived.wait_recv()
                copy.start()

    def y_start(half):
        for k in range(1, 4):
            y_copy(half, k).start()

    def after_y(half):
        total = s_x[half * 4 + y].astype(jnp.float32)
        for k in range(1, 4):
            y_copy(half, k).wait_recv()
            total = total + r_y[half, k - 1].astype(jnp.float32)
        s_z[half] = total.astype(jnp.bfloat16)
        zl_copy(half).start()

    def settle(half):
        zl_copy(half).wait_recv()
        total = s_z[half].astype(jnp.float32) + r_z[half].astype(jnp.float32)
        change = whole_global[half] - total * (1.0 / 64)
        delta[half] = change
        full[1, half, y, x, c] = change.astype(jnp.bfloat16)
        near_start(1, half)

    def early_near():
        for copy in early_copies():
            copy.wait_recv()
        near_start(0, 0)
        near_start(0, 1)

    def early_far():
        far_start(0, 0)
        far_start(0, 1)

    def early_across():
        across_start(0, 0)
        across_start(0, 1)

    whole_global[zl] = global_own[...]
    base = global_own[...] - (outer_rate * outer_beta * outer_beta) * momentum_own[...]
    full[0, zl, y, x, c] = base.astype(jnp.bfloat16)
    d_normed[...] = jnp.zeros_like(d_normed)
    for copy in early_copies():
        copy.start()
    def sum_a():
        change = delta[zl]
        squares = jnp.sum((change * change).reshape(4, 8, WIDTH), axis=0)
        folded = squares[:, :128]
        for first in range(128, WIDTH, 128):
            folded = folded + squares[:, first : first + 128]
        sq_a[x, c] = folded
        for copy in a_copies:
            copy.start()

    def sum_b():
        for copy in a_copies:
            copy.wait_recv()
        sq_b[y] = jnp.sum(sq_a[...].reshape(8, 8, 128), axis=0)
        for copy in b_copies:
            copy.start()

    def sum_c():
        for copy in b_copies:
            copy.wait_recv()
        sq_c[zl, j] = jnp.sum(sq_b[...], axis=0)
        for copy in c_copies:
            copy.start()

    def apply(half, share):
        for k in range(4):
            for which in range(2):
                for copy in across_copies(which, half, k):
                    copy.wait_recv()

        @pl.loop(0, 16)
        def _(i):
            row, column = lax.div(i, 4), lax.rem(i, 4)
            base = full[0, half, row, column].astype(jnp.float32)
            moved = base - share * full[1, half, row, column].astype(jnp.float32)
            new_weight[half, row, column] = moved.astype(jnp.bfloat16)

    def finish():
        for copy in c_copies:
            copy.wait_recv()
        square_sum = jnp.sum(jnp.sum(sq_c[...].reshape(8, 8, 128), axis=0), keepdims=True)
        factor = jnp.minimum(1.0, clip_rms / jnp.sqrt(square_sum / ENTRIES + 1e-06))
        clipped = factor * delta[zl]
        moment = outer_beta * momentum_own[...] + clipped
        new_momentum[...] = moment
        new_global[...] = global_own[...] - outer_rate * (clipped + outer_beta * moment)
        share[...] = jnp.broadcast_to(factor * (outer_rate * (1.0 + outer_beta)), share.shape)

    def backward(g):
        backward_group(
            *[g, a_log, dt_bias, skip, d_normed, gated, z_ref, tables],
            *[b_ref, c_ref, dt_ref, gain_ref, grad_x],
        )

    a_copies = [
        remote(sq_a.at[x, c], sq_a.at[x, c], a_send.at[i], a_recv.at[i], on_x(*peer))
        for i, peer in enumerate(x_peers)
    ]
    b_copies = [
        remote(sq_b.at[y], sq_b.at[y], b_send.at[k - 1], b_recv.at[k - 1], on_y(k))
        for k in range(1, 4)
    ]
    c_copies = [
        remote(sq_c.at[zl, j], sq_c.at[zl, j], c_send.at[i], c_recv.at[i], on_z(*peer))
        for i, peer in enumerate(z_peers)
    ]
    actions = {
        "begin": begin,
        "pass": pass_on,
        "own": own,
        "relay": relay,
        "grad": gradients,
        "ox": over_x,
        "ax": after_x,
        "early_near": early_near,
        "early_far": early_far,
        "early_across": early_across,
        "ys": y_start,
        "ay": after_y,
        "se": settle,
        "far": lambda half: far_start(1, half),
        "ac": lambda half: across_start(1, half),
        "a": sum_a,
        "b": sum_b,
        "c": sum_c,
        "fin": finish,
        "bwd": backward,
    }
    for name, *index in ORDER:
        actions[name](*index)
    for half in range(2):
        apply(half, share[0:1, 0:1])

    for copy in [*a_copies, *b_copies, *c_copies, *early_copies()]:
        copy.wait_send()
    for half in range(2):
        zl_copy(half).wait_send()
        for k in range(1, 4):
            y_copy(half, k).wait_send()
        for which in range(2):
            for copy in near_copies(which, half):
                copy.wait_send()
            for k in range(4):
                for copy in across_copies(which, half, k):
                    copy.wait_send()
                if k:
                    for copy in far_copies(which, half, k):
                        copy.wait_send()

    for u in range(UNITS):
        for kind in KINDS:
            z_copy(kind, u).wait_send()
        core_copy(u).wait_send()
        for k in range(1, 4):
            x_copy(u, k).wait_send()


def step(a_log, dt_bias, skip, x_in, gate_z, b_proj, c_proj, dt, gain, weight, target, *outer):
    half = jnp.bfloat16
    piece = (UNITS, TOKENS, FEATURES)
    dma = pltpu.SemaphoreType.DMA
    vmem = pl.BlockSpec(memory_space=pltpu.VMEM)
    smem = pl.BlockSpec(memory_space=pltpu.SMEM)
    grad_x, new_weight, new_global, new_momentum = pl.pallas_call(
        step_kernel,
        out_shape=(
            jax.ShapeDtypeStruct((512, WIDTH), half),
            jax.ShapeDtypeStruct((2, 4, 4, 2, 32, WIDTH), half),
            jax.ShapeDtypeStruct((32, WIDTH), jnp.float32),
            jax.ShapeDtypeStruct((32, WIDTH), jnp.float32),
        ),
        in_specs=[*[smem] * 3, *[vmem] * 6, pl.BlockSpec(memory_space=pl.ANY), *[vmem] * 3],
        out_specs=[vmem] * 4,
        scratch_shapes=[
            pltpu.VMEM((2048, WIDTH), half),
            pltpu.VMEM((512, WIDTH), half),
            pltpu.VMEM((512, WIDTH), jnp.float32),
            pltpu.VMEM((2, 2, 8, SPAN, SPAN), half),
            pltpu.VMEM((512, WIDTH), jnp.float32),
            pltpu.VMEM((2, 2, 4, 4, 2, 32, WIDTH), half),
            pltpu.VMEM((UNITS, 4, TOKENS, FEATURES), jnp.float32),
            *[pltpu.VMEM(piece, half)] * 6,
            pltpu.VMEM((UNITS, 4, TOKENS, FEATURES), half),
            pltpu.VMEM((UNITS, 4, 2, 32, WIDTH), half),
            pltpu.VMEM((UNITS, 4, 32, WIDTH), half),
            pltpu.VMEM((UNITS, 4, 32, WIDTH), half),
            pltpu.VMEM((UNITS, 3, 32, WIDTH), half),
            pltpu.VMEM((UNITS, 32, WIDTH), half),
            pltpu.VMEM((2, 3, 32, WIDTH), half),
            pltpu.VMEM((2, 32, WIDTH), half),
            pltpu.VMEM((2, 32, WIDTH), half),
            pltpu.VMEM((2, 32, WIDTH), jnp.float32),
            pltpu.VMEM((2, 32, WIDTH), jnp.float32),
            pltpu.VMEM((4, 2, 8, 128), jnp.float32),
            pltpu.VMEM((4, 8, 128), jnp.float32),
            pltpu.VMEM((2, 4, 8, 128), jnp.float32),
            pltpu.VMEM((8, 128), jnp.float32),
            dma,
            *[dma((UNITS, len(KINDS)))] * 2,
            *[dma((UNITS,))] * 2,
            *[dma((UNITS, 3))] * 2,
            *[dma((2, 3))] * 2,
            *[dma((2,))] * 2,
            *[dma((2,))] * 2,
            *[dma((7,))] * 2,
            *[dma((3,))] * 2,
            *[dma((7,))] * 2,
            *[dma((4, 20))] * 2,
        ],
        compiler_params=pltpu.CompilerParams(
            collective_id=0, has_side_effects=True, vmem_limit_bytes=67043328
        ),
    )(a_log, dt_bias, skip, x_in, gate_z, b_proj, c_proj, dt, gain, weight, target, *outer)
    return grad_x, new_weight.reshape(2048, WIDTH), new_global, new_momentum


def shards(
    x_in,
    gate_z,
    b_proj,
    c_proj,
    dt_raw,
    a_log,
    dt_bias,
    skip_d,
    norm_gain,
    out_weight,
    global_weight,
    momentum,
    target,
):
    return step(
        *[a_log, dt_bias, skip_d, x_in, gate_z, b_proj, c_proj, dt_raw.T],
        *[norm_gain.reshape(1, WIDTH), out_weight[0], target, global_weight, momentum],
    )


def solution(mesh):
    torus = Mesh(
        mesh.devices.reshape(2, 4, 4, 2, mesh.shape["tensor"]),
        ("replica_0", "replica_1", "replica_2", "replica_3", "tensor"),
    )
    in_specs = (
        P(REPLICA, "tensor"),
        P(REPLICA, "tensor"),
        P(REPLICA, "tensor"),
        P(REPLICA, "tensor"),
        P(REPLICA, "tensor"),
        P("tensor"),
        P("tensor"),
        P("tensor"),
        P("tensor"),
        P(REPLICA, None, "tensor"),
        P(REPLICA, "tensor"),
        P(REPLICA, "tensor"),
        P(REPLICA_TENSOR, None),
    )
    out_specs = (
        P(REPLICA, "tensor"),
        P(None, "tensor"),
        P(REPLICA, "tensor"),
        P(REPLICA, "tensor"),
    )
    return jax.shard_map(
        shards, mesh=torus, in_specs=in_specs, out_specs=out_specs, check_vma=False
    )
```

time: 240 us -> 152 us (0.63)
  local copies, waits for them, and re-layouts: 53.8 us -> 8.26 us
  other arithmetic: 21 us -> 0 us
  matrix products: 16.3 us -> 0 us
  Pallas kernels: 147 us -> 143 us
    reshape x14 -> x0, local copies, waits for them, and re-layouts: 33.7 us -> none  [the longest x3 12.6 us: gated_ssd(): ssd_out.reshape(tokens, group_count, width)]
    dot_general x7 -> x0, matrix products: 16.3 us -> none  [the longest x2 9.6 us: gated_ssd(): inside = jnp.einsum('cgrls,csgrp->clgrp', weights, values)]
    mul x3 -> x0, other arithmetic: 8.04 us -> none  [the longest x1 3.31 us: gated_ssd(): (gated_vals * inv_norm).reshape(tokens, head_count * HEAD_DIM) * norm_gain]
    pallas_call x1, Pallas kernels: 147 us -> 143 us  [step(): pl.pallas_call(step_kernel, out_shape=(jax.ShapeDtypeStruct((512, WIDTH),...]
    unnamed x38 -> x8, local copies, waits for them, and re-layouts: 13 us -> 8.26 us
    reduce_sum x1 -> x0, other arithmetic: 3.39 us -> none  [gated_ssd(): gated_vals * inv_norm]
    add x1 -> x0, local copies, waits for them, and re-layouts: 2.96 us -> none  [gated_ssd(): inside + outside]
    mul x8 -> x0, local copies, waits for them, and re-layouts: 2.84 us -> none  [the longest x1 1.92 us: gated_ssd(): jax.nn.silu(gate_z.astype(jnp.float32)).reshape(tokens, group_count, width)]
where the time goes in v4:
time: 152 us; the launch traced here: 151 us
  Pallas kernels  143 us (94%)
  local copies, waits for them, and re-layouts  8.26 us (5%)
    pallas_call x1, Pallas kernels, step(): pl.pallas_call(step_kernel, out_shape=(jax.ShapeDtypeStruct((512, WIDTH),...  143 us
    unnamed x8, local copies, waits for them, and re-layouts  8.26 us

profile of v4, /device:TPU:1, one launch (start us, length us, event | category | flops | bytes accessed | tf_op | source)
XLA Modules:
  0.0 151.5 jit_solution(2881726739254472175)
XLA Ops:
  0.6 142.6 %shard_map.156 = (bf16[512,1024]{1,0:T(8,128)(2,1)}, bf16[2,4,4,2,32,1024]{5,4,3,2,1,0:T(8,128)(2,1)}, f32[32,1024]{1,0:T(8,128)}, f32[32,1024]{1,0:T(8,128)}) custom-call(f32[16]{0:T(128)} %a_log.1, f32[16]{0:T(128)} %dt_bias.1, f32[16]{0:T(128)} %skip.1, bf16[512,1024]{1,0:T(8,128)(2,1)} %x_ref.1, bf16[512,1024]{1,0:T(8,128)(2,1)} %z_ref.1, ...), custom_call_target="tpu_custom_call" | custom-call | tf_op jit(solution)/shard_map/pallas_call | solution.py:692
  143.2 2.3 %copy.21 = bf16[512,1024]{1,0:T(8,128)(2,1)} copy(bf16[512,1024]{1,0:T(8,128)(2,1)} %get-tuple-element.16) | data formatting | bytes 2097152
  145.5 0.0 copy-start.1
  145.5 0.0 copy-start
  145.5 4.7 %copy.22 = bf16[2048,1024]{1,0:T(8,128)(2,1)} copy(bf16[2048,1024]{1,0:T(8,128)(2,1)} %bitcast.5) | data formatting | bytes 8388608
  150.2 0.0 copy-done.1
  150.2 0.7 copy.23
  150.8 0.0 copy-done
  150.8 0.7 copy.24
Async XLA Ops:
  145.5 4.7 %copy-start.1 = (f32[32,1024]{1,0:T(8,128)S(1)}, f32[32,1024]{1,0:T(8,128)}, u32[]{:S(2)}) copy-start(f32[32,1024]{1,0:T(8,128)} %get-tuple-element.18) | copy-start | bytes 393220
  145.5 5.3 %copy-start = (f32[32,1024]{1,0:T(8,128)S(1)}, f32[32,1024]{1,0:T(8,128)}, u32[]{:S(2)}) copy-start(f32[32,1024]{1,0:T(8,128)} %get-tuple-element.19) | copy-start | bytes 393220

commit v5 on v4

--- a/solution.py
+++ b/solution.py
@@ -28,78 +28,80 @@
     ("begin", 0),
     ("begin", 1),
     ("begin", 2),
+    ("pass", 0),
+    ("early_near",),
+    ("pass", 1),
     ("begin", 3),
+    ("pass", 2),
     ("begin", 4),
-    ("pass", 0),
+    ("own", 0),
+    ("own", 1),
+    ("pass", 3),
+    ("early_far",),
+    ("own", 2),
+    ("relay", 0),
+    ("pass", 4),
+    ("relay", 1),
+    ("own", 3),
+    ("relay", 2),
+    ("grad", 0),
     ("begin", 5),
     ("begin", 6),
-    ("pass", 2),
-    ("early_near",),
+    ("ox", 0),
+    ("grad", 1),
     ("begin", 7),
-    ("pass", 1),
-    ("pass", 4),
-    ("early_far",),
-    ("own", 0),
-    ("pass", 3),
-    ("pass", 6),
-    ("own", 2),
+    ("relay", 3),
+    ("ox", 1),
+    ("grad", 2),
+    ("own", 4),
+    ("ox", 2),
+    ("ax", 0),
     ("pass", 5),
     ("early_across",),
-    ("own", 4),
+    ("ax", 1),
+    ("pass", 6),
     ("pass", 7),
-    ("own", 1),
+    ("ax", 2),
+    ("relay", 4),
+    ("grad", 3),
+    ("ox", 3),
+    ("own", 5),
     ("own", 6),
-    ("relay", 0),
-    ("own", 3),
-    ("relay", 2),
-    ("own", 5),
-    ("relay", 1),
-    ("relay", 4),
     ("own", 7),
-    ("relay", 3),
+    ("out", 0),
     ("relay", 5),
-    ("grad", 1),
+    ("grad", 4),
+    ("ax", 3),
+    ("ys", 0),
+    ("ox", 4),
     ("relay", 6),
-    ("grad", 0),
     ("relay", 7),
-    ("ox", 1),
-    ("grad", 3),
-    ("ox", 0),
-    ("grad", 2),
-    ("ox", 3),
-    ("ax", 1),
+    ("ay", 0),
     ("grad", 5),
-    ("ox", 2),
-    ("ax", 0),
-    ("grad", 4),
+    ("ax", 4),
     ("ox", 5),
-    ("ax", 3),
+    ("grad", 6),
     ("grad", 7),
-    ("ox", 4),
-    ("ax", 2),
-    ("ys", 0),
-    ("grad", 6),
+    ("ox", 6),
     ("ox", 7),
+    ("se", 0),
+    ("bwd", 0),
+    ("ax", 5),
     ("bwd", 1),
-    ("ox", 6),
-    ("ay", 0),
-    ("ax", 4),
-    ("ax", 5),
-    ("bwd", 0),
-    ("se", 0),
+    ("ax", 6),
     ("ax", 7),
-    ("ax", 6),
     ("ys", 1),
     ("far", 0),
     ("ay", 1),
     ("se", 1),
     ("a",),
     ("ac", 0),
+    ("far", 1),
     ("b",),
-    ("far", 1),
+    ("out", 1),
+    ("ac", 1),
     ("c",),
     ("fin",),
-    ("ac", 1),
 )
 
 
@@ -149,11 +151,10 @@
     g, a_log, dt_bias, skip, x_all, z_all, b_all, c_all, dt_all, gain_all, normed, gated_all, tables
 ):
     first = g * 8
-    wide = pl.ds(pl.multiple_of(g * 512, 512), 512)
-    narrow = pl.ds(pl.multiple_of(g * STATE, STATE), STATE)
+    wide, narrow = slice(g * 512, g * 512 + 512), slice(g * STATE, g * STATE + STATE)
     x_ref, z_ref = x_all.at[:, wide], z_all.at[:, wide]
     b_ref, c_ref = b_all.at[:, narrow], c_all.at[:, narrow]
-    dt_ref = dt_all.at[pl.ds(pl.multiple_of(first, 8), 8)]
+    dt_ref = dt_all.at[first : first + 8]
     gain_ref, normed_ref, gated_ref = gain_all.at[:, wide], normed.at[:, wide], gated_all.at[:, wide]
     below, steps, by_row, by_column = decays(dt_ref, a_log, dt_bias, first)
     low = lax.broadcasted_iota(jnp.int32, (1, 128), 1) < HEAD_DIM
@@ -249,7 +250,8 @@
     global_own,
     momentum_own,
     grad_x,
-    new_weight,
+    pair,
+    share,
     new_global,
     new_momentum,
     weight,
@@ -279,8 +281,8 @@
     sq_a,
     sq_b,
     sq_c,
-    share,
     weight_sem,
+    out_sem,
     z_send,
     z_recv,
     core_send,
@@ -329,15 +331,14 @@
     fetch = pltpu.make_async_copy(weight_in, weight, weight_sem)
     fetch.start()
 
-    @pl.loop(0, 2)
-    def _(g):
+    def forward(g):
         forward_group(
             *[g, a_log, dt_bias, skip, x_ref, z_ref, b_ref, c_ref, dt_ref, gain_ref],
             *[normed, gated, tables],
         )
 
+    forward(0)
     pl.semaphore_wait(barrier, len(z_peers) + len(x_peers) + 3)
-    fetch.wait()
 
     def remote(src, dst, send_sem, recv_sem, device):
         return pltpu.make_async_remote_copy(
@@ -566,6 +567,8 @@
     d_normed[...] = jnp.zeros_like(d_normed)
     for copy in early_copies():
         copy.start()
+    forward(1)
+    fetch.wait()
     def sum_a():
         change = delta[zl]
         squares = jnp.sum((change * change).reshape(4, 8, WIDTH), axis=0)
@@ -590,18 +593,19 @@
         for copy in c_copies:
             copy.start()
 
-    def apply(half, share):
-        for k in range(4):
-            for which in range(2):
+    def out_copies(index):
+        if index == 0:
+            return [pltpu.make_async_copy(full.at[0], pair.at[0], out_sem.at[0])]
+        half = index - 1
+        return [pltpu.make_async_copy(full.at[1, half], pair.at[1, half], out_sem.at[index])]
+
+    def out(index):
+        for which, half in (((0, 0), (0, 1)) if index == 0 else ((1, index - 1),)):
+            for k in range(4):
                 for copy in across_copies(which, half, k):
                     copy.wait_recv()
-
-        @pl.loop(0, 16)
-        def _(i):
-            row, column = lax.div(i, 4), lax.rem(i, 4)
-            base = full[0, half, row, column].astype(jnp.float32)
-            moved = base - share * full[1, half, row, column].astype(jnp.float32)
-            new_weight[half, row, column] = moved.astype(jnp.bfloat16)
+        for copy in out_copies(index):
+            copy.start()
 
     def finish():
         for copy in c_copies:
@@ -653,12 +657,15 @@
         "c": sum_c,
         "fin": finish,
         "bwd": backward,
+        "out": out,
     }
     for name, *index in ORDER:
         actions[name](*index)
-    for half in range(2):
-        apply(half, share[0:1, 0:1])
-
+    out(2)
+
+    for index in range(3):
+        for copy in out_copies(index):
+            copy.wait()
     for copy in [*a_copies, *b_copies, *c_copies, *early_copies()]:
         copy.wait_send()
     for half in range(2):
@@ -683,22 +690,59 @@
             x_copy(u, k).wait_send()
 
 
+def apply_kernel(pair, share, grad_in, global_in, momentum_in, grad, weight, new_global, moment):
+    grad[...] = grad_in[...]
+    new_global[...] = global_in[...]
+    moment[...] = momentum_in[...]
+    factor = share[0:1, 0:1]
+
+    @pl.loop(0, 8)
+    def _(i):
+        part = pl.ds(pl.multiple_of(i * 64, 64), 64)
+        base = pair[0, part].astype(jnp.float32)
+        weight[part] = (base - factor * pair[1, part].astype(jnp.float32)).astype(jnp.bfloat16)
+
+
+def apply(pair, share, grad_x, new_global, new_momentum):
+    slim = pl.BlockSpec((128, WIDTH), lambda i: (i, 0))
+    rows = pl.BlockSpec((32, 256), lambda i: (0, i))
+    grad, weight, new_global, new_momentum = pl.pallas_call(
+        apply_kernel,
+        grid=(4,),
+        out_shape=(
+            jax.ShapeDtypeStruct((512, WIDTH), jnp.bfloat16),
+            jax.ShapeDtypeStruct((2048, WIDTH), jnp.bfloat16),
+            jax.ShapeDtypeStruct((32, WIDTH), jnp.float32),
+            jax.ShapeDtypeStruct((32, WIDTH), jnp.float32),
+        ),
+        in_specs=[
+            pl.BlockSpec((2, 512, WIDTH), lambda i: (0, i, 0)),
+            pl.BlockSpec((8, 128), lambda i: (0, 0)),
+            *[slim, rows, rows],
+        ],
+        out_specs=[slim, pl.BlockSpec((512, WIDTH), lambda i: (i, 0)), rows, rows],
+        compiler_params=pltpu.CompilerParams(vmem_limit_bytes=67043328),
+    )(pair, share, grad_x, new_global, new_momentum)
+    return grad, weight, new_global, new_momentum
+
+
 def step(a_log, dt_bias, skip, x_in, gate_z, b_proj, c_proj, dt, gain, weight, target, *outer):
     half = jnp.bfloat16
     piece = (UNITS, TOKENS, FEATURES)
     dma = pltpu.SemaphoreType.DMA
     vmem = pl.BlockSpec(memory_space=pltpu.VMEM)
     smem = pl.BlockSpec(memory_space=pltpu.SMEM)
-    grad_x, new_weight, new_global, new_momentum = pl.pallas_call(
+    grad_x, pair, share, new_global, new_momentum = pl.pallas_call(
         step_kernel,
         out_shape=(
             jax.ShapeDtypeStruct((512, WIDTH), half),
-            jax.ShapeDtypeStruct((2, 4, 4, 2, 32, WIDTH), half),
+            jax.ShapeDtypeStruct((2, 2, 4, 4, 2, 32, WIDTH), half),
+            jax.ShapeDtypeStruct((8, 128), jnp.float32),
             jax.ShapeDtypeStruct((32, WIDTH), jnp.float32),
             jax.ShapeDtypeStruct((32, WIDTH), jnp.float32),
         ),
         in_specs=[*[smem] * 3, *[vmem] * 6, pl.BlockSpec(memory_space=pl.ANY), *[vmem] * 3],
-        out_specs=[vmem] * 4,
+        out_specs=[vmem, pl.BlockSpec(memory_space=pl.ANY), *[vmem] * 3],
         scratch_shapes=[
             pltpu.VMEM((2048, WIDTH), half),
             pltpu.VMEM((512, WIDTH), half),
@@ -722,8 +766,8 @@
             pltpu.VMEM((4, 2, 8, 128), jnp.float32),
             pltpu.VMEM((4, 8, 128), jnp.float32),
             pltpu.VMEM((2, 4, 8, 128), jnp.float32),
-            pltpu.VMEM((8, 128), jnp.float32),
             dma,
+            dma((3,)),
             *[dma((UNITS, len(KINDS)))] * 2,
             *[dma((UNITS,))] * 2,
             *[dma((UNITS, 3))] * 2,
@@ -739,7 +783,7 @@
             collective_id=0, has_side_effects=True, vmem_limit_bytes=67043328
         ),
     )(a_log, dt_bias, skip, x_in, gate_z, b_proj, c_proj, dt, gain, weight, target, *outer)
-    return grad_x, new_weight.reshape(2048, WIDTH), new_global, new_momentum
+    return apply(pair.reshape(2, 2048, WIDTH), share, grad_x, new_global, new_momentum)
 
 
 def shards(

time: 152 us -> 140 us (0.921)
  local copies, waits for them, and re-layouts: 8.26 us -> 0 us
  Pallas kernels: 143 us -> 138 us
    pallas_call x1, Pallas kernels: 143 us -> 131 us  [step(): pl.pallas_call(step_kernel, out_shape=(jax.ShapeDtypeStruct((512, WIDTH),...]
    unnamed x8 -> x0, local copies, waits for them, and re-layouts: 8.26 us -> none
    pallas_call x0 -> x1, Pallas kernels: none -> 7.32 us  [apply(): pl.pallas_call(apply_kernel, grid=(4,), out_shape=(jax.ShapeDtypeStruct((...]
where the time goes in v5:
time: 140 us; the launch traced here: 139 us
  Pallas kernels  138 us (99%)
    pallas_call x1, Pallas kernels, step(): pl.pallas_call(step_kernel, out_shape=(jax.ShapeDtypeStruct((512, WIDTH),...  131 us
    pallas_call x1, Pallas kernels, apply(): pl.pallas_call(apply_kernel, grid=(4,), out_shape=(jax.ShapeDtypeStruct((...  7.32 us

profile of v5, /device:TPU:1, one launch (start us, length us, event | category | flops | bytes accessed | tf_op | source)
XLA Modules:
  0.0 139.0 jit_solution(7081643897530886029)
XLA Ops:
  0.6 130.8 %shard_map.156 = (bf16[512,1024]{1,0:T(8,128)(2,1)}, bf16[2,2,4,4,2,32,1024]{6,5,4,3,2,1,0:T(8,128)(2,1)}, f32[8,128]{1,0:T(8,128)}, f32[32,1024]{1,0:T(8,128)}, f32[32,1024]{1,0:T(8,128)}) custom-call(f32[16]{0:T(128)} %a_log.1, f32[16]{0:T(128)} %dt_bias.1, f32[16]{0:T(128)} %skip.1, bf16[512,1024]{1,0:T(8,128)(2,1)} %x_ref.1, bf16[512,1024]{1,0:T(8,128)(2,1)} %z_ref.1, ...), custom_call_target="tpu_custom_call" | custom-call | tf_op jit(solution)/shard_map/pallas_call | solution.py:735
  131.5 7.3 %shard_map.157 = (bf16[512,1024]{1,0:T(8,128)(2,1)}, bf16[2048,1024]{1,0:T(8,128)(2,1)}, f32[32,1024]{1,0:T(8,128)}, f32[32,1024]{1,0:T(8,128)}) custom-call(bf16[2,2048,1024]{2,1,0:T(8,128)(2,1)} %bitcast.4, f32[8,128]{1,0:T(8,128)} %get-tuple-element.10.share, bf16[512,1024]{1,0:T(8,128)(2,1)} %get-tuple-element.11.grad_in, ...), custom_call_target="tpu_custom_call" | custom-call | tf_op jit(solution)/shard_map/pallas_call | solution.py:709

commit v6 on v5

--- a/solution.py
+++ b/solution.py
@@ -39,8 +39,8 @@
     ("pass", 3),
     ("early_far",),
     ("own", 2),
+    ("pass", 4),
     ("relay", 0),
-    ("pass", 4),
     ("relay", 1),
     ("own", 3),
     ("relay", 2),
@@ -53,41 +53,41 @@
     ("relay", 3),
     ("ox", 1),
     ("grad", 2),
+    ("early_across",),
+    ("pass", 5),
+    ("ox", 2),
     ("own", 4),
-    ("ox", 2),
     ("ax", 0),
-    ("pass", 5),
-    ("early_across",),
+    ("pass", 6),
     ("ax", 1),
-    ("pass", 6),
     ("pass", 7),
     ("ax", 2),
+    ("grad", 3),
+    ("own", 5),
     ("relay", 4),
-    ("grad", 3),
     ("ox", 3),
-    ("own", 5),
     ("own", 6),
     ("own", 7),
     ("out", 0),
     ("relay", 5),
-    ("grad", 4),
     ("ax", 3),
     ("ys", 0),
-    ("ox", 4),
+    ("grad", 4),
     ("relay", 6),
     ("relay", 7),
+    ("ox", 4),
     ("ay", 0),
     ("grad", 5),
-    ("ax", 4),
     ("ox", 5),
     ("grad", 6),
     ("grad", 7),
     ("ox", 6),
     ("ox", 7),
     ("se", 0),
+    ("ax", 4),
+    ("bwd", 1),
+    ("ax", 5),
     ("bwd", 0),
-    ("ax", 5),
-    ("bwd", 1),
     ("ax", 6),
     ("ax", 7),
     ("ys", 1),
@@ -96,11 +96,11 @@
     ("se", 1),
     ("a",),
     ("ac", 0),
+    ("b",),
     ("far", 1),
-    ("b",),
     ("out", 1),
+    ("c",),
     ("ac", 1),
-    ("c",),
     ("fin",),
 )
 
@@ -159,6 +159,7 @@
     below, steps, by_row, by_column = decays(dt_ref, a_log, dt_bias, first)
     low = lax.broadcasted_iota(jnp.int32, (1, 128), 1) < HEAD_DIM
     tails = tail_keys(b_ref[:SPAN], steps[0], by_row[0])
+    corner = below[: SPAN // 2, : SPAN // 2]
     for k in range(2):
         rows = slice(k * SPAN, (k + 1) * SPAN)
         scores = dot(c_ref[rows], b_ref[rows], (1, 1))
@@ -168,11 +169,19 @@
             values = x_ref[rows, cols]
             sides = []
             for r in (2 * q, 2 * q + 1):
-                gap = by_column[k][:, r : r + 1] - by_row[k][r : r + 1]
-                table = jnp.where(below, jnp.exp(gap), 0.0)
-                weights = (scores * table * steps[k][r : r + 1]).astype(jnp.bfloat16)
-                tables[g, k, r] = weights
-                sides.append(dot(weights, values, (1, 0)))
+                late, early = by_column[k][:, r : r + 1], by_row[k][r : r + 1]
+                step = steps[k][r : r + 1]
+                for top in (0, SPAN // 2):
+                    own = slice(top, top + SPAN // 2)
+                    table = jnp.where(corner, jnp.exp(late[own] - early[:, own]), 0.0)
+                    weights = scores[own, own] * table * step[:, own]
+                    tables[g, k, r, own, own] = weights.astype(jnp.bfloat16)
+                lower, upper = slice(SPAN // 2, SPAN), slice(0, SPAN // 2)
+                table = jnp.exp(late[lower] - early[:, upper])
+                weights = scores[lower, upper] * table * step[:, upper]
+                tables[g, k, r, lower, upper] = weights.astype(jnp.bfloat16)
+                tables[g, k, r, upper, lower] = jnp.zeros((SPAN // 2, SPAN // 2), jnp.bfloat16)
+                sides.append(dot(tables[g, k, r], values, (1, 0)))
             skips = paired(low, skip[first + 2 * q], skip[first + 2 * q + 1])
             out = paired(low, *sides) + skips * values.astype(jnp.float32)
             if k == 1:
@@ -440,25 +449,30 @@
         whole = cot[u].reshape(4 * TOKENS, FEATURES)
         for first in range(0, WIDTH, 512):
             cols = slice(first, first + 512)
-            rows = weight[rows_of(u), cols]
             grad = lax.dot_general(
                 whole,
                 normed[:, cols],
                 (((0,), (0,)), ((), ())),
                 preferred_element_type=jnp.float32,
             )
-            moved = (rows.astype(jnp.float32) - inner_rate * grad).astype(jnp.bfloat16)
+            rows = weight[rows_of(u), cols].astype(jnp.float32)
+            moved = (rows - inner_rate * grad).astype(jnp.bfloat16)
             fresh[u, :, :, :, cols] = moved.reshape(4, 2, 32, 512)
-            d_normed[:, cols] += jnp.dot(whole, rows, preferred_element_type=jnp.float32)
         core_copy(u).start()
+        for first in range(0, WIDTH, 512):
+            cols = slice(first, first + 512)
+            d_normed[:, cols] += jnp.dot(
+                whole, weight[rows_of(u), cols], preferred_element_type=jnp.float32
+            )
 
     def over_x(u):
         core_copy(u).wait_recv()
-        for i in range(4):
+        for k in (2, 1, 3, 0):
+            i = lax.rem(x + k, 4)
             both = fresh[u, i, c].astype(jnp.float32) + r_core[u, i].astype(jnp.float32)
             s_core[u, i] = both.astype(jnp.bfloat16)
-        for k in range(1, 4):
-            x_copy(u, k).start()
+            if k:
+                x_copy(u, k).start()
 
     def after_x(u):
         total = s_core[u, x].astype(jnp.float32)
@@ -696,7 +710,7 @@
     moment[...] = momentum_in[...]
     factor = share[0:1, 0:1]
 
-    @pl.loop(0, 8)
+    @pl.loop(0, 16)
     def _(i):
         part = pl.ds(pl.multiple_of(i * 64, 64), 64)
         base = pair[0, part].astype(jnp.float32)
@@ -704,11 +718,11 @@
 
 
 def apply(pair, share, grad_x, new_global, new_momentum):
-    slim = pl.BlockSpec((128, WIDTH), lambda i: (i, 0))
-    rows = pl.BlockSpec((32, 256), lambda i: (0, i))
+    slim = pl.BlockSpec((256, WIDTH), lambda i: (i, 0))
+    rows = pl.BlockSpec((32, 512), lambda i: (0, i))
     grad, weight, new_global, new_momentum = pl.pallas_call(
         apply_kernel,
-        grid=(4,),
+        grid=(2,),
         out_shape=(
             jax.ShapeDtypeStruct((512, WIDTH), jnp.bfloat16),
             jax.ShapeDtypeStruct((2048, WIDTH), jnp.bfloat16),
@@ -716,11 +730,11 @@
             jax.ShapeDtypeStruct((32, WIDTH), jnp.float32),
         ),
         in_specs=[
-            pl.BlockSpec((2, 512, WIDTH), lambda i: (0, i, 0)),
+            pl.BlockSpec((2, 1024, WIDTH), lambda i: (0, i, 0)),
             pl.BlockSpec((8, 128), lambda i: (0, 0)),
             *[slim, rows, rows],
         ],
-        out_specs=[slim, pl.BlockSpec((512, WIDTH), lambda i: (i, 0)), rows, rows],
+        out_specs=[slim, pl.BlockSpec((1024, WIDTH), lambda i: (i, 0)), rows, rows],
         compiler_params=pltpu.CompilerParams(vmem_limit_bytes=67043328),
     )(pair, share, grad_x, new_global, new_momentum)
     return grad, weight, new_global, new_momentum

time: 140 us -> 137 us (0.979)
  Pallas kernels: 138 us -> 136 us
    pallas_call x1, Pallas kernels: 131 us -> 129 us  [step(): pl.pallas_call(step_kernel, out_shape=(jax.ShapeDtypeStruct((512, WIDTH),...]
where the time goes in v6:
time: 137 us
  Pallas kernels  136 us (99%)
    pallas_call x1, Pallas kernels, step(): pl.pallas_call(step_kernel, out_shape=(jax.ShapeDtypeStruct((512, WIDTH),...  129 us
    pallas_call x1, Pallas kernels, apply(): pl.pallas_call(apply_kernel, grid=(2,), out_shape=(jax.ShapeDtypeStruct((...  6.51 us

profile of v6, /device:TPU:1, one launch (start us, length us, event | category | flops | bytes accessed | tf_op | source)
XLA Modules:
  0.0 136.7 jit_solution(5855719417222241888)
XLA Ops:
  0.6 129.4 %shard_map.156 = (bf16[512,1024]{1,0:T(8,128)(2,1)}, bf16[2,2,4,4,2,32,1024]{6,5,4,3,2,1,0:T(8,128)(2,1)}, f32[8,128]{1,0:T(8,128)}, f32[32,1024]{1,0:T(8,128)}, f32[32,1024]{1,0:T(8,128)}) custom-call(f32[16]{0:T(128)} %a_log.1, f32[16]{0:T(128)} %dt_bias.1, f32[16]{0:T(128)} %skip.1, bf16[512,1024]{1,0:T(8,128)(2,1)} %x_ref.1, bf16[512,1024]{1,0:T(8,128)(2,1)} %z_ref.1, ...), custom_call_target="tpu_custom_call" | custom-call | tf_op jit(solution)/shard_map/pallas_call | solution.py:749
  130.0 6.5 %shard_map.157 = (bf16[512,1024]{1,0:T(8,128)(2,1)}, bf16[2048,1024]{1,0:T(8,128)(2,1)}, f32[32,1024]{1,0:T(8,128)}, f32[32,1024]{1,0:T(8,128)}) custom-call(bf16[2,2048,1024]{2,1,0:T(8,128)(2,1)} %bitcast.4, f32[8,128]{1,0:T(8,128)} %get-tuple-element.10.share, bf16[512,1024]{1,0:T(8,128)(2,1)} %get-tuple-element.11.grad_in, ...), custom_call_target="tpu_custom_call" | custom-call | tf_op jit(solution)/shard_map/pallas_call | solution.py:723
